TPU v7x, 512 devices: a whole 4x8x8 slice. The times are simulated.
512 devices in a mesh: dom: 128 (over y, z, core), scen: 4 (over x).
Axes of the slice: x: 4, y: 8, z: 8, core: 2. Of those that a mesh axis runs over, the one named last changes fastest.
Arguments:
- embedding: bfloat16 [1310720, 256], P(('dom', 'scen')), may hold values from -6 to 6
- scenario_feats: bfloat16 [16, 1310720], P(None, ('dom', 'scen')), may hold values from -6 to 6
- adjacency: bfloat16 [10240, 2, 128, 128], P(('dom', 'scen')), may hold values from -0.3125 to 0.3125
- driver_weight: bfloat16 [1310720, 128], P(('dom', 'scen')), may hold values from -0.3125 to 0.3125
- local_slot: int32 [10240], P(('dom', 'scen')), may hold values from 0 to 79, as said below
- halo_slot: int32 [10240], P(('dom', 'scen')), may hold values from 0 to 15, as said below
- send_rows: int32 [65536, 16], P(('dom', 'scen')), may hold values from 0 to 2559
- send_count: int32 [65536], P(('dom', 'scen')), may hold values from 1 to 16, as said below
- hot_ids: int32 [128], replicated, may hold values from 0 to 1310719, as said below
- first_weight: bfloat16 [512, 256], P('scen'), may hold values from -0.25 to 0.25
- feature_weight: bfloat16 [16, 256], replicated, may hold values from -1.5 to 1.5
- first_bias: float32 [256], replicated, may hold values from -3 to 3
- second_weight: bfloat16 [256, 256], P('scen'), may hold values from -0.375 to 0.375
- second_bias: float32 [256], replicated, may hold values from -3 to 3
Outputs:
- updated: bfloat16 [1310720, 256], P(('dom', 'scen'))
Inputs may be any that keep to these rules, and one draw needn't show every extreme that they name: `local_slot`: the 20 entries of one device are distinct and name exactly 5 tiles of each device of its partition; values s * 20 to s * 20 + 19 are tiles of scen index s. `halo_slot`: the entries of one device name every halo tile at least once. `send_count`: every device has a partition to which it sends 16 pins. `hot_ids`: no device holds more than 1 of them, and some device holds exactly that many.
All inputs are finite; a program needn't handle non-finite values.
Results may differ from a plain program's by a relative error of at most 0.0038.
Values may be sent and summed in bfloat16 or wider, within the bound.
No kernel may reach another device: no remote copies, remote signals or barrier semaphores. Data moves between devices by JAX's collectives and lax.ppermute only.
A program may use at most 64 MiB of HBM per device.

v0:
```python
import jax
import jax.numpy as jnp
from jax import lax
from jax.sharding import PartitionSpec as P


def per_device(
    embedding,
    scenario_feats,
    adjacency,
    driver_weight,
    local_slot,
    halo_slot,
    send_rows,
    send_count,
    hot_ids,
    first_weight,
    feature_weight,
    first_bias,
    second_weight,
    second_bias,
):
    rows, width = embedding.shape
    tile = adjacency.shape[-1]
    tiles = rows // tile
    groups = lax.axis_size("scen")
    partition = lax.all_gather(embedding, "scen", axis=0, tiled=True)
    local_tiles = partition.reshape(groups * tiles, tile, width)[local_slot]
    slots_per_peer = send_rows.shape[1]
    live = jnp.arange(slots_per_peer, dtype=jnp.int32)[None, :] < send_count[:, None]
    outgoing_rows = jnp.where(
        live[:, :, None], embedding[send_rows], jnp.zeros((), embedding.dtype)
    )
    incoming = lax.all_to_all(outgoing_rows, "dom", split_axis=0, concat_axis=0, tiled=True)
    halo_tiles = incoming.reshape(-1, tile, width)[halo_slot]
    myself = lax.axis_index(("dom", "scen"))
    owner = hot_ids // rows
    within = hot_ids - owner * rows
    mine = jnp.where(
        (owner == myself)[:, None], embedding[within].astype(jnp.float32), jnp.float32(0.0)
    )
    drivers = lax.psum(mine, ("dom", "scen")).astype(jnp.bfloat16)
    summed = jnp.einsum(
        "tij,tjc->tic", adjacency[:, 0], local_tiles, preferred_element_type=jnp.float32
    )
    summed = summed + jnp.einsum(
        "tij,tjc->tic", adjacency[:, 1], halo_tiles, preferred_element_type=jnp.float32
    )
    summed = summed.reshape(rows, width) + jnp.dot(
        driver_weight, drivers, preferred_element_type=jnp.float32
    )
    aggregate = summed.astype(jnp.bfloat16)
    joined = jnp.concatenate([embedding, aggregate], axis=1)
    starting = (
        jnp.dot(scenario_feats.T, feature_weight, preferred_element_type=jnp.float32) + first_bias
    )
    columns = joined
    inner = starting + jnp.dot(
        columns,
        lax.all_gather(first_weight, "scen", axis=0, tiled=True),
        preferred_element_type=jnp.float32,
    )
    activated = jax.nn.gelu(inner, approximate=False).astype(jnp.bfloat16)
    residual = embedding.astype(jnp.float32) + second_bias
    columns = activated
    result = residual + jnp.dot(
        columns,
        lax.all_gather(second_weight, "scen", axis=0, tiled=True),
        preferred_element_type=jnp.float32,
    )
    return result.astype(jnp.bfloat16)


def solution(mesh):
    return jax.shard_map(
        per_device,
        mesh=mesh,
        in_specs=(
            P(("dom", "scen"), None),
            P(None, ("dom", "scen")),
            P(("dom", "scen"), None, None, None),
            P(("dom", "scen"), None),
            P(("dom", "scen")),
            P(("dom", "scen")),
            P(("dom", "scen"), None),
            P(("dom", "scen")),
            P(),
            P("scen", None),
            P(),
            P(),
            P("scen", None),
            P(),
        ),
        out_specs=P(("dom", "scen"), None),
        check_vma=False,
    )
```

profile of v0, /device:TPU:16, one launch (start us, length us, event | category | flops | bytes accessed | tf_op | source)
XLA Modules:
  0.0 204.4 jit_solution(11013594092646320890)
XLA Ops:
  6.5 0.0 copy-start
  6.5 0.0 copy-start.1
  6.5 0.0 all-gather.2.cloned.1.call-start
  6.5 0.7 all-gather.2.cloned.1.call-update
  7.3 0.7 compare_select_fusion
  8.0 0.1 copy.18
  8.1 0.1 reshape.46
  8.2 0.0 copy-done.1
  8.2 0.0 copy-start.6
  8.2 7.5 %gather_fusion.1 = bf16[2048,256]{1,0:T(8,128)(2,1)S(1)} fusion(bf16[2560,256]{1,0:T(8,128)(2,1)S(1)} %copy-done.1, s32[2048]{0:T(1024)S(1)} %broadcast_clamp_fusion), kind=kCustom, calls=%fused_computation.1 | custom fusion | bytes 2105344 | tf_op jit(solution)/shard_map/gather | solution.py:32
  15.7 0.0 copy-done.6
  15.7 0.0 copy-start.7
  15.7 0.1 iota_compare_fusion
  15.8 0.0 copy-start.5
  15.8 0.0 copy-start.4
  15.8 1.2 broadcast_select_fusion
  17.1 17.4 %all-to-all-start = ((bf16[128,16,256]{2,1,0:T(8,128)(2,1)}), bf16[128,16,256]{2,1,0:T(8,128)(2,1)S(1)}, u32[]{:S(2)}, u32[]{:S(2)}) async-start(bf16[128,16,256]{2,1,0:T(8,128)(2,1)} %broadcast_select_fusion), calls=%async_computation | async-start | bytes 2097152 | tf_op jit(solution)/shard_map/all_to_all | solution.py:34
  34.4 0.0 copy-done.7
  34.5 0.8 gather_fusion.3
  35.3 0.1 convert_select_fusion
  35.4 114.3 %all-reduce.1 = bf16[128,256]{1,0:T(8,128)(2,1)S(1)} all-reduce(f32[128,256]{1,0:T(8,128)S(1)} %convert_select_fusion), channel_id=1, replica_groups=mesh['dom'=128,'scen'=4] {'dom','scen'}, use_global_device_ids=true, to_apply=%region_0.1 | all-reduce | flops 32768 | bytes 196608 | tf_op jit(solution)/shard_map/psum | solution.py:42
  149.7 12.2 %all_gather.11 = bf16[256,256]{1,0:T(8,128)(2,1)S(1)} all-gather(bf16[64,256]{1,0:T(8,128)(2,1)} %param.26), channel_id=1, replica_groups=mesh['dom'=128,'scen'=4] {'scen'}, dimensions={0}, use_global_device_ids=true | all-gather | bytes 163840 | tf_op jit(solution)/shard_map/all_gather | solution.py:68
  161.9 0.0 copy-done.5
  161.9 13.2 %all_gather.10 = bf16[512,256]{1,0:T(8,128)(2,1)} all-gather(bf16[128,256]{1,0:T(8,128)(2,1)S(1)} %copy-done.5), channel_id=1, replica_groups=mesh['dom'=128,'scen'=4] {'scen'}, dimensions={0}, use_global_device_ids=true | all-gather | bytes 327680 | tf_op jit(solution)/shard_map/all_gather | solution.py:60
  175.1 0.7 compare_select_fusion.2
  175.8 0.7 compare_select_fusion.3
  176.4 0.6 pad_clamp_fusion.2
  177.0 0.0 copy-done.4
  177.0 2.7 %convolution_add_fusion.2 = f32[2560,256]{1,0:T(8,128)} fusion(bf16[16,2560]{1,0:T(8,128)(2,1)S(1)} %copy-done.4, bf16[16,256]{1,0:T(8,128)(2,1)} %param.24, f32[256]{0:T(256)} %param.25), kind=kOutput, calls=%fused_computation.6 | convolution fusion | flops 21626880 | bytes 2712576 | tf_op jit(solution)/shard_map/dot_general | solution.py:55
  179.8 0.0 all-to-all-done
  179.8 1.8 gather_fusion.2
  181.5 0.0 all-gather.2.cloned.1.call-done
  181.5 3.2 %gather_fusion = bf16[20,128,256]{2,1,0:T(8,128)(2,1)S(1)} fusion(bf16[80,128,256]{2,1,0:T(8,128)(2,1)} %bitcast.33, s32[1024]{0:T(1024)} %pad_clamp_fusion.2), kind=kCustom, calls=%fused_computation | custom fusion | bytes 2621520 | tf_op jit(solution)/shard_map/gather | solution.py:28
  184.8 0.0 copy-start.2
  184.8 0.0 copy-start.3
  184.8 1.7 fusion.52
  186.5 0.0 copy-done.2
  186.5 0.1 copy-done.3
  186.7 0.5 convolution_add_fusion.3
  187.2 0.0 copy-start.8
  187.2 0.0 copy-done
  187.2 0.5 fusion.1
  187.7 0.2 copy-done.8
  187.9 9.7 %fusion.2 = bf16[2560,256]{1,0:T(8,128)(2,1)} fusion(bf16[256,256]{1,0:T(8,128)(2,1)S(1)} %all_gather.11, bf16[2560,256]{1,0:T(8,128)(2,1)S(1)} %copy-done.1, f32[256]{0:T(256)S(1)} %copy-done.8, f32[2560,256]{1,0:T(8,128)} %convolution_add_fusion.2, bf16[512,256]{1,0:T(8,128)(2,1)} %all_gather.10, bf16[2560,256]{1,0:T(8,128)(2,1)S(1)} %fusion.1), kind=kOutput, calls=%fused_computation.11 | convolution fusion | flops 1057751040 | bytes 6947840 | tf_op jit(solution)/shard_map/dot_general | solution.py:66
  (5 shorter events, 0.0 us)
Async XLA Ops:
  6.5 180.7 %copy-start = (bf16[2560,128]{1,0:T(8,128)(2,1)S(1)}, bf16[2560,128]{1,0:T(8,128)(2,1)}, u32[]{:S(2)}) copy-start(bf16[2560,128]{1,0:T(8,128)(2,1)} %param.17) | copy-start | bytes 1966084
  6.5 1.6 copy-start.1
  6.5 175.0 %all-gather.2.cloned.1.call-start = ((), (), s32[]{:S(2)}) async-start(), calls=%async_computation.1 | async-start | bytes 6553600 | tf_op jit(solution)/shard_map/all_gather | solution.py:27
  8.2 7.5 %copy-start.6 = (s32[128]{0:T(128)S(1)}, s32[128]{0:T(128)}, u32[]{:S(2)}) copy-start(s32[128]{0:T(128)} %param.21) | copy-start | bytes 1540
  15.7 18.7 %copy-start.7 = (s32[128]{0:T(128)S(1)}, s32[128]{0:T(128)}, u32[]{:S(2)}) copy-start(s32[128]{0:T(128)} %param.22) | copy-start | bytes 1540
  15.8 146.1 %copy-start.5 = (bf16[128,256]{1,0:T(8,128)(2,1)S(1)}, bf16[128,256]{1,0:T(8,128)(2,1)}, u32[]{:S(2)}) copy-start(bf16[128,256]{1,0:T(8,128)(2,1)} %param.23) | copy-start | bytes 196612
  15.8 161.2 %copy-start.4 = (bf16[16,2560]{1,0:T(8,128)(2,1)S(1)}, bf16[16,2560]{1,0:T(8,128)(2,1)}, u32[]{:S(2)}) copy-start(bf16[16,2560]{1,0:T(8,128)(2,1)} %param.15) | copy-start | bytes 245764
  17.1 162.7 %all-to-all-start = ((bf16[128,16,256]{2,1,0:T(8,128)(2,1)}), bf16[128,16,256]{2,1,0:T(8,128)(2,1)S(1)}, u32[]{:S(2)}, u32[]{:S(2)}) async-start(bf16[128,16,256]{2,1,0:T(8,128)(2,1)} %broadcast_select_fusion), calls=%async_computation | async-start | bytes 2097152 | tf_op jit(solution)/shard_map/all_to_all | solution.py:34
  184.8 1.8 copy-start.2
  184.8 1.9 copy-start.3
  187.2 0.7 copy-start.8
Sparse Core Ops, SparseCore 0:
  9.5 66.7 all-gather.1
where the time goes:
time: 205 us; the launch traced here: 204 us
  blocking collectives  140 us (68%)
  starting transfers between devices  17.4 us (8%)
  matrix products  15.1 us (7%)
  local copies, waits for them, and re-layouts  13.9 us (7%)
  between operations  13.6 us (7%)
  other arithmetic  4.05 us (2%)
    psum x1, blocking collectives, per_device(): drivers = lax.psum(mine, ('dom', 'scen')).astype(jnp.bfloat16)  114 us
    all_to_all x1, starting transfers between devices, per_device(): lax.all_to_all(outgoing_rows, 'dom', split_axis=0, concat_axis=0, tiled=T...  17.4 us
    all_gather x1, blocking collectives, per_device(): lax.all_gather(first_weight, 'scen', axis=0, tiled=True)  13.2 us
    all_gather x1, blocking collectives, per_device(): lax.all_gather(second_weight, 'scen', axis=0, tiled=True)  12.2 us
    dot_general x1, matrix products, per_device(): jnp.dot(columns, lax.all_gather(second_weight, 'scen', axis=0, tiled=True...  9.68 us
    gather x1, local copies, waits for them, and re-layouts, per_device(): embedding[send_rows]  7.5 us
  transfers between devices with their start and end apart: 2, of which 0 were waited for; matrix products, arithmetic and copies ran while one was open for 8% of the time, Pallas kernels for 0%

commit v1 on v0

v1 whole, which is shorter than its diff:
```python
import jax
import jax.numpy as jnp
from jax import lax
from jax.experimental import pallas as pl
from jax.experimental.pallas import tpu as pltpu
from jax.sharding import PartitionSpec as P

BF16, F32, I32 = jnp.bfloat16, jnp.float32, jnp.int32
VMEM_BYTES = 48 * 1024 * 1024
NOTE = 16


def _params(**more):
    return pltpu.CompilerParams(vmem_limit_bytes=VMEM_BYTES, **more)


def _dot(a, b):
    return jnp.dot(a, b, preferred_element_type=F32)


def note(myself, hot_ids, local_slot, embedding, groups):
    rows, width = embedding.shape
    hots, tiles = hot_ids.shape[0], local_slot.shape[0]

    def body(myself_ref, hot_ref, slot_ref, emb_ref, out_ref, block, page, sem):
        within = hot_ref[...] - myself_ref[0] * rows
        row = jnp.max(jnp.where((within >= 0) & (within < rows), within, -1))
        start = pl.multiple_of((jnp.maximum(row, 0) // NOTE) * NOTE, NOTE)
        copy = pltpu.make_async_copy(emb_ref.at[pl.ds(start, NOTE), :], block, sem)
        copy.start()
        page[...] = jnp.zeros((NOTE, width), F32)
        page[1:2, :tiles] = slot_ref[...].astype(F32)
        copy.wait()
        at = lax.broadcasted_iota(I32, (NOTE, width), 0)
        mine = jnp.where(at == row - start, block[...].astype(F32), 0.0)
        page[0:1, :] = jnp.sum(mine, axis=0, keepdims=True)
        out_ref[...] = jnp.broadcast_to(page[...].astype(BF16)[None], (groups, NOTE, width))

    return pl.pallas_call(
        body,
        out_shape=jax.ShapeDtypeStruct((groups, NOTE, width), BF16),
        in_specs=[
            pl.BlockSpec(memory_space=pltpu.SMEM),
            pl.BlockSpec((1, hots), lambda: (0, 0)),
            pl.BlockSpec((1, tiles), lambda: (0, 0)),
            pl.BlockSpec(memory_space=pl.ANY),
        ],
        out_specs=pl.BlockSpec((groups, NOTE, width), lambda: (0, 0, 0)),
        scratch_shapes=[
            pltpu.VMEM((NOTE, width), BF16),
            pltpu.VMEM((NOTE, width), F32),
            pltpu.SemaphoreType.DMA(()),
        ],
        compiler_params=_params(),
        name="note",
    )(myself, hot_ids.reshape(1, hots), local_slot.reshape(1, tiles), embedding)


def pick_rows(send_rows, send_count, embedding):
    rows, width = embedding.shape
    doms, cap = send_rows.shape
    half = width // 2
    step = 32
    parts = rows // 128

    def body(rows_ref, count_ref, emb_ref, out_ref, chosen):
        slot = lax.broadcasted_iota(I32, (cap, doms), 0)
        index = jnp.where(slot < count_ref[...], rows_ref[...], -1)
        lane = lax.broadcasted_iota(I32, (cap, 128), 1).astype(F32).astype(BF16)
        one, zero = jnp.ones((), BF16), jnp.zeros((), BF16)

        def some(i, _):
            turned = pltpu.roll(index, (doms - i * step) % doms, 1)
            low = (turned & 127).astype(F32)
            high = (turned >> 7).astype(F32)
            for p in range(step):
                low_p = jnp.broadcast_to(low[:, p : p + 1], (cap, 128)).astype(BF16)
                high_p = jnp.broadcast_to(high[:, p : p + 1], (cap, 128)).astype(BF16)
                at = jnp.where(low_p == lane, one, zero)
                for k in range(parts):
                    chosen[p * cap : (p + 1) * cap, k * 128 : (k + 1) * 128] = jnp.where(
                        high_p == jnp.asarray(k, BF16), at, zero
                    )
            got = _dot(chosen[...], emb_ref[...]).astype(BF16).reshape(step, cap, width)
            here = pl.ds(pl.multiple_of(i * step, step), step)
            out_ref[here, :cap, :] = got[:, :, :half]
            out_ref[here, cap : 2 * cap, :] = got[:, :, half:]
            out_ref[here, 2 * cap :, :] = jnp.zeros((step, 8, half), BF16)
            return 0

        lax.fori_loop(0, doms // step, some, 0)

    return pl.pallas_call(
        body,
        out_shape=jax.ShapeDtypeStruct((doms, 2 * cap + 8, half), BF16),
        in_specs=[
            pl.BlockSpec((cap, doms), lambda: (0, 0)),
            pl.BlockSpec((1, doms), lambda: (0, 0)),
            pl.BlockSpec((rows, width), lambda: (0, 0)),
        ],
        out_specs=pl.BlockSpec((doms, 2 * cap + 8, half), lambda: (0, 0, 0)),
        scratch_shapes=[pltpu.VMEM((step * cap, rows), BF16)],
        compiler_params=_params(),
        name="pick_rows",
    )(send_rows.T, send_count.reshape(1, doms), embedding)


def add_drivers(notes, message):
    doms, length, half = message.shape
    groups = notes.shape[0]

    def body(notes_ref, _, out_ref, page, sem):
        at = lax.broadcasted_iota(I32, (8, half), 0)
        last = jnp.zeros((8, half), F32)
        for g in range(groups):
            row = notes_ref[g].astype(F32)[0:1, :]
            last = jnp.where(at == g, row[:, :half], last)
            last = jnp.where(at == groups + g, row[:, half:], last)
        page[...] = jnp.broadcast_to(last[None], (doms, 8, half)).astype(BF16)
        copy = pltpu.make_async_copy(page, out_ref.at[:, pl.ds(length - 8, 8), :], sem)
        copy.start()
        copy.wait()

    return pl.pallas_call(
        body,
        out_shape=jax.ShapeDtypeStruct(message.shape, BF16),
        in_specs=[pl.BlockSpec(notes.shape, lambda: (0, 0, 0)), pl.BlockSpec(memory_space=pl.ANY)],
        out_specs=pl.BlockSpec(memory_space=pl.ANY),
        scratch_shapes=[pltpu.VMEM((doms, 8, half), BF16), pltpu.SemaphoreType.DMA(())],
        input_output_aliases={1: 0},
        compiler_params=_params(),
        name="add_drivers",
    )(notes, message)


def pick_tiles(group, slots, embedding, first_weight, second_weight, tile):
    groups, tiles = slots.shape
    rows, width = embedding.shape
    each = tiles // groups
    a, b = first_weight.shape[0], second_weight.shape[0]
    length = each * tile + a + b

    def body(group_ref, slots_ref, emb_ref, first_ref, second_ref, *rest):
        outs, (listed, sems) = rest[: groups - 1], rest[groups - 1 :]
        me = group_ref[0]
        copies = []
        for k in range(1, groups):
            out = outs[k - 1]
            other = (me + k) % groups
            copies.append(pltpu.make_async_copy(first_ref, out.at[pl.ds(each * tile, a), :], sems.at[k - 1, each]))
            copies.append(
                pltpu.make_async_copy(second_ref, out.at[pl.ds(each * tile + a, b), :], sems.at[k - 1, each + 1])
            )
            for j in range(each):
                listed[k - 1, j] = 0

            def look(t, found, k=k, other=other):
                tile_at = slots_ref[other, t]
                hit = tile_at // tiles == me

                @pl.when(hit)
                def _():
                    listed[k - 1, jnp.minimum(found, each - 1)] = tile_at - me * tiles

                return found + hit.astype(I32)

            lax.fori_loop(0, tiles, look, jnp.zeros((), I32))
            for j in range(each):
                start = pl.multiple_of(listed[k - 1, j] * tile, tile)
                copies.append(
                    pltpu.make_async_copy(
                        emb_ref.at[pl.ds(start, tile), :], out.at[pl.ds(j * tile, tile), :], sems.at[k - 1, j]
                    )
                )
        for copy in copies:
            copy.start()
        for copy in copies:
            copy.wait()

    hbm = pl.BlockSpec(memory_space=pl.ANY)
    smem = pl.BlockSpec(memory_space=pltpu.SMEM)
    return pl.pallas_call(
        body,
        out_shape=[jax.ShapeDtypeStruct((length, width), BF16)] * (groups - 1),
        in_specs=[smem, smem, hbm, hbm, hbm],
        out_specs=[hbm] * (groups - 1),
        scratch_shapes=[
            pltpu.SMEM((groups - 1, each), I32),
            pltpu.SemaphoreType.DMA((groups - 1, each + 2)),
        ],
        compiler_params=_params(),
        name="pick_tiles",
    )(group, slots, embedding, first_weight, second_weight)


def before_halo(
    group, slot, embedding, arrived, first_weight, second_weight, adjacency, feats, feature_weight, first_bias
):
    rows, width = embedding.shape
    tiles, _, tile, _ = adjacency.shape
    groups = len(arrived) + 1
    each = tiles // groups
    a, b = first_weight.shape[0], second_weight.shape[0]
    many = 2
    block = many * tile

    def body(group_ref, slot_ref, emb_ref, own_a, own_b, adj_ref, feat_ref, fw_ref, bias_ref, *rest):
        parts = rest[: groups - 1]
        local_ref, start_ref, lower_ref, second_ref, weight, got, place = rest[groups - 1 :]
        me = group_ref[0]
        i = pl.program_id(0)

        @pl.when(i == 0)
        def _():
            mine_a, mine_b = pl.ds(pl.multiple_of(me * a, a), a), pl.ds(pl.multiple_of(me * b, b), b)
            weight[mine_a, :] = own_a[...]
            second_ref[mine_b, :] = own_b[...]
            for k in range(1, groups):
                other = (me + groups - k) % groups
                there_a = pl.ds(pl.multiple_of(other * a, a), a)
                there_b = pl.ds(pl.multiple_of(other * b, b), b)
                weight[there_a, :] = parts[k - 1][each * tile : each * tile + a, :]
                second_ref[there_b, :] = parts[k - 1][each * tile + a :, :]
            lower_ref[...] = weight[width:, :]

            def number(t, counts):
                source = slot_ref[t] // tiles
                spot = sum(jnp.where(source == g, counts[g], 0) for g in range(groups))
                place[t] = spot
                return tuple(counts[g] + (source == g).astype(I32) for g in range(groups))

            lax.fori_loop(0, tiles, number, (jnp.zeros((), I32),) * groups)

        for u in range(many):
            t = i * many + u
            source = slot_ref[t] // tiles
            away = (me + groups - source) % groups

            @pl.when(away == 0)
            def _():
                at = pl.multiple_of((slot_ref[t] - source * tiles) * tile, tile)
                got[...] = emb_ref[pl.ds(at, tile), :]

            for k in range(1, groups):

                @pl.when(away == k)
                def _(k=k):
                    at = pl.multiple_of(jnp.minimum(place[t], each - 1) * tile, tile)
                    got[...] = parts[k - 1][pl.ds(at, tile), :]

            local_ref[u * tile : (u + 1) * tile, :] = _dot(adj_ref[u, 0], got[...])
        own = emb_ref[pl.ds(pl.multiple_of(i * block, block), block), :]
        start_ref[...] = (
            _dot(own, weight[:width, :])
            + lax.dot_general(feat_ref[...], fw_ref[...], (((0,), (0,)), ((), ())), preferred_element_type=F32)
            + bias_ref[...]
        )

    def whole(x):
        return pl.BlockSpec(x.shape, lambda i, *_: (0,) * x.ndim)

    f32_rows = jax.ShapeDtypeStruct((rows, width), F32)
    square = jax.ShapeDtypeStruct((width, width), BF16)
    by_rows = pl.BlockSpec((block, width), lambda i, *_: (i, 0))
    fixed = pl.BlockSpec((width, width), lambda i, *_: (0, 0))
    return pl.pallas_call(
        body,
        out_shape=[f32_rows, f32_rows, square, square],
        grid_spec=pltpu.PrefetchScalarGridSpec(
            num_scalar_prefetch=2,
            grid=(tiles // many,),
            in_specs=[
                whole(embedding),
                whole(first_weight),
                whole(second_weight),
                pl.BlockSpec((many, 1, tile, tile), lambda i, *_: (i, 0, 0, 0)),
                pl.BlockSpec((feats.shape[0], block), lambda i, *_: (0, i)),
                whole(feature_weight),
                whole(first_bias),
                *[whole(x) for x in arrived],
            ],
            out_specs=[by_rows, by_rows, fixed, fixed],
            scratch_shapes=[
                pltpu.VMEM((2 * width, width), BF16),
                pltpu.VMEM((tile, width), BF16),
                pltpu.SMEM((tiles,), I32),
            ],
        ),
        compiler_params=_params(),
        name="before_halo",
    )(group, slot, embedding, first_weight, second_weight, adjacency, feats, feature_weight, first_bias, *arrived)


def after_halo(
    halo_slot, halo, driver_at, local, start, adjacency, driver_weight, embedding, lower, second, second_bias
):
    rows, width = embedding.shape
    tiles, _, tile, _ = adjacency.shape
    doms, length, half = halo.shape
    cap = (length - 8) // 2
    hots = driver_weight.shape[1]
    many = 2
    block = many * tile
    per = tile // cap

    def body(
        slot_ref, halo_ref, at_ref, local_ref, start_ref, adj_ref, dw_ref, emb_ref, lower_ref, second_ref, bias_ref,
        out_ref, drivers, summed,
    ):
        i = pl.program_id(0)

        @pl.when(i == 0)
        def _():
            column = lax.broadcasted_iota(I32, (hots, doms * 8), 1)
            ends = halo_ref[:, 2 * cap :, :].reshape(doms * 8, half)
            left = jnp.where(column == at_ref[...], 1.0, 0.0).astype(BF16)
            right = jnp.where(column == at_ref[...] + 4, 1.0, 0.0).astype(BF16)
            drivers[:, :half] = _dot(left, ends).astype(BF16)
            drivers[:, half:] = _dot(right, ends).astype(BF16)

        for u in range(many):
            which = pl.ds(pl.multiple_of(slot_ref[i * many + u] * per, per), per)
            here = slice(u * tile, (u + 1) * tile)
            summed[here, :half] = local_ref[here, :half] + _dot(
                adj_ref[u, 0], halo_ref[which, :cap, :].reshape(tile, half)
            )
            summed[here, half:] = local_ref[here, half:] + _dot(
                adj_ref[u, 0], halo_ref[which, cap : 2 * cap, :].reshape(tile, half)
            )
        aggregate = (summed[...] + _dot(dw_ref[...], drivers[...])).astype(BF16)
        inner = start_ref[...] + _dot(aggregate, lower_ref[...])
        activated = (0.5 * inner * (1.0 + lax.erf(inner * (0.5**0.5)))).astype(BF16)
        out_ref[...] = (emb_ref[...].astype(F32) + bias_ref[...] + _dot(activated, second_ref[...])).astype(BF16)

    def whole(x):
        return pl.BlockSpec(x.shape, lambda i, *_: (0,) * x.ndim)

    by_rows = pl.BlockSpec((block, width), lambda i, *_: (i, 0))
    return pl.pallas_call(
        body,
        out_shape=jax.ShapeDtypeStruct((rows, width), BF16),
        grid_spec=pltpu.PrefetchScalarGridSpec(
            num_scalar_prefetch=1,
            grid=(tiles // many,),
            in_specs=[
                whole(halo),
                whole(driver_at),
                by_rows,
                by_rows,
                pl.BlockSpec((many, 1, tile, tile), lambda i, *_: (i, 1, 0, 0)),
                pl.BlockSpec((block, hots), lambda i, *_: (i, 0)),
                by_rows,
                whole(lower),
                whole(second),
                whole(second_bias),
            ],
            out_specs=by_rows,
            scratch_shapes=[pltpu.VMEM((hots, width), BF16), pltpu.VMEM((block, width), F32)],
        ),
        compiler_params=_params(),
        name="after_halo",
    )(halo_slot, halo, driver_at, local, start, adjacency, driver_weight, embedding, lower, second, second_bias)


def per_device(
    embedding,
    scenario_feats,
    adjacency,
    driver_weight,
    local_slot,
    halo_slot,
    send_rows,
    send_count,
    hot_ids,
    first_weight,
    feature_weight,
    first_bias,
    second_weight,
    second_bias,
):
    rows, width = embedding.shape
    tile = adjacency.shape[-1]
    tiles = rows // tile
    groups = lax.axis_size("scen")
    myself = lax.axis_index(("dom", "scen")).astype(I32).reshape(1)
    group = lax.axis_index("scen").astype(I32).reshape(1)

    page = note(myself, hot_ids, local_slot, embedding, groups)
    notes = lax.all_to_all(page, "scen", split_axis=0, concat_axis=0, tiled=True)
    message = pick_rows(send_rows, send_count, embedding)
    message = add_drivers(notes, message)
    halo = lax.all_to_all(message, "dom", split_axis=0, concat_axis=0, tiled=True)

    slots = notes[:, 1, :tiles].astype(I32)
    leaving = pick_tiles(group, slots, embedding, first_weight, second_weight, tile)
    arrived = [
        lax.ppermute(x, "scen", [(g, (g + k) % groups) for g in range(groups)])
        for k, x in enumerate(leaving, start=1)
    ]
    local, start, lower, second = before_halo(
        group,
        local_slot,
        embedding,
        arrived,
        first_weight,
        second_weight,
        adjacency,
        scenario_feats,
        feature_weight,
        first_bias.reshape(1, width),
    )
    owner = hot_ids // rows
    driver_at = (owner // groups * 8 + owner % groups).reshape(-1, 1)
    return after_halo(
        halo_slot,
        halo,
        driver_at,
        local,
        start,
        adjacency,
        driver_weight,
        embedding,
        lower,
        second,
        second_bias.reshape(1, width),
    )


def solution(mesh):
    return jax.shard_map(
        per_device,
        mesh=mesh,
        in_specs=(
            P(("dom", "scen"), None),
            P(None, ("dom", "scen")),
            P(("dom", "scen"), None, None, None),
            P(("dom", "scen"), None),
            P(("dom", "scen")),
            P(("dom", "scen")),
            P(("dom", "scen"), None),
            P(("dom", "scen")),
            P(),
            P("scen", None),
            P(),
            P(),
            P("scen", None),
            P(),
        ),
        out_specs=P(("dom", "scen"), None),
        check_vma=False,
    )
```

time: 205 us -> 90.2 us (0.44)
  the two profiles are of different devices: /device:TPU:16 before, /device:TPU:19 now
where the time goes in v1:
time: 90.2 us; the launch traced here: 89.4 us
  starting transfers between devices  32.6 us (36%)
  Pallas kernels  29.2 us (32%)
  waiting for transfers between devices  14.7 us (16%)
  local copies, waits for them, and re-layouts  12.1 us (13%)
    all_to_all x1, starting transfers between devices, per_device(): lax.all_to_all(message, 'dom', split_axis=0, concat_axis=0, tiled=True)  18.8 us
    ppermute x3, waiting for transfers between devices, per_device(): lax.ppermute(x, 'scen', [(g, (g + k) % groups) for g in range(groups)])  14.6 us
    unnamed x50, local copies, waits for them, and re-layouts  10.8 us
    pallas_call x1, Pallas kernels, after_halo(): pl.pallas_call(body, out_shape=jax.ShapeDtypeStruct((rows, width), BF16),...  10.7 us
    ppermute x3, starting transfers between devices, per_device(): lax.ppermute(x, 'scen', [(g, (g + k) % groups) for g in range(groups)])  9.59 us
    pallas_call x1, Pallas kernels, before_halo(): pl.pallas_call(body, out_shape=[f32_rows, f32_rows, square, square], grid...  8.6 us
    pallas_call x1, Pallas kernels, pick_rows(): pl.pallas_call(body, out_shape=jax.ShapeDtypeStruct((doms, 2 * cap + 8, h...  5.23 us
    all_to_all x1, starting transfers between devices, per_device(): lax.all_to_all(page, 'scen', split_axis=0, concat_axis=0, tiled=True)  4.28 us
  transfers between devices with their start and end apart: 5, of which 3 were waited for; matrix products, arithmetic and copies ran while one was open for 2% of the time, Pallas kernels for 19%

profile of v1, /device:TPU:19, one launch (start us, length us, event | category | flops | bytes accessed | tf_op | source)
XLA Modules:
  0.0 89.4 jit_solution(9330208756689141235)
XLA Ops:
  0.0 0.0 copy-start.24
  0.0 0.0 copy-start.15
  0.0 0.0 copy-start
  0.0 1.3 %copy-done = bf16[2560,256]{1,0:T(8,128)(2,1)S(1)} copy-done((bf16[2560,256]{1,0:T(8,128)(2,1)S(1)}, bf16[2560,256]{1,0:T(8,128)(2,1)}, u32[]{:S(2)}) %copy-start) | copy-done | bytes 1310744
  1.3 0.0 copy-start.17
  1.4 0.7 copy-done.17
  2.0 0.0 copy-start.21
  2.0 0.7 copy-done.21
  2.7 0.0 copy-start.1
  2.7 0.9 note.1
  3.5 4.3 %all-to-all-start = ((bf16[4,16,256]{2,1,0:T(8,128)(2,1)}), bf16[4,16,256]{2,1,0:T(8,128)(2,1)S(1)}, u32[]{:S(2)}, u32[]{:S(2)}) async-start(bf16[4,16,256]{2,1,0:T(8,128)(2,1)} %note.1), calls=%async_computation | async-start | bytes 65536 | tf_op jit(solution)/shard_map/all_to_all | solution.py:389
  7.8 0.0 copy-done.24
  7.8 0.0 copy-done.15
  7.8 0.0 copy-done.1
  7.8 5.2 %pick_rows.1._ = bf16[128,40,128]{2,1,0:T(8,128)(2,1)} custom-call(s32[16,128]{1,0:T(8,128)S(1)} %bitcast.11, s32[1,128]{1,0:T(1,128)S(1)} %bitcast.17, bf16[2560,256]{1,0:T(8,128)(2,1)S(1)} %copy-done.1), custom_call_target="tpu_custom_call" | custom-call | tf_op jit(solution)/shard_map/pick_rows/pallas_call | solution.py:93
  13.0 0.0 all-to-all-done.notes_ref
  13.0 0.7 add_drivers.1
  13.8 0.0 copy-start.8
  13.8 0.0 copy-start.12
  13.8 18.8 %all-to-all-start.1 = ((bf16[128,40,128]{2,1,0:T(8,128)(2,1)}), bf16[128,40,128]{2,1,0:T(8,128)(2,1)}, u32[]{:S(2)}, u32[]{:S(2)}) async-start(bf16[128,40,128]{2,1,0:T(8,128)(2,1)} %add_drivers.1), calls=%async_computation.1 | async-start | bytes 2621440 | tf_op jit(solution)/shard_map/all_to_all | solution.py:392
  32.6 0.0 copy-start.22
  32.6 0.0 copy-start.2
  32.6 0.0 copy-start.16
  32.6 0.0 copy-start.18
  32.6 0.0 copy-start.19
  32.7 0.0 copy-done.8
  32.7 0.0 copy-done.12
  32.7 3.1 %pick_tiles.1 = (bf16[832,256]{1,0:T(8,128)(2,1)}, bf16[832,256]{1,0:T(8,128)(2,1)}, bf16[832,256]{1,0:T(8,128)(2,1)}) custom-call(s32[1]{0:T(128)} %bitcast.6.group_ref, s32[4,20]{1,0:T(4,128)S(1)} %bitcast.12, bf16[2560,256]{1,0:T(8,128)(2,1)S(1)} %copy-done.1, bf16[128,256]{1,0:T(8,128)(2,1)S(1)} %copy-done.8, bf16[64,256]{1,0:T(8,128)(2,1)S(1)} %copy-done.12), custom_call_target="tpu_custom_call" | custom-call | tf_op jit(solution)/shard_map/pick_tiles/pallas_call | solution.py:182
  35.8 3.1 %collective-permute-start = (bf16[832,256]{1,0:T(8,128)(2,1)}, bf16[832,256]{1,0:T(8,128)(2,1)S(1)}, u32[]{:S(2)}, u32[]{:S(2)}) collective-permute-start(bf16[832,256]{1,0:T(8,128)(2,1)} %get-tuple-element.12), channel_id=1, source_target_pairs={{0,1},{1,2},{2,3},{3,0},{4,5},{5,6},{6,7},{7,4},{8,9},{9,10},{10,1... | collective-permute-start | bytes 1277960 | tf_op jit(solution)/shard_map/ppermute | solution.py:397
  38.9 2.5 %collective-permute-start.1 = (bf16[832,256]{1,0:T(8,128)(2,1)}, bf16[832,256]{1,0:T(8,128)(2,1)S(1)}, u32[]{:S(2)}, u32[]{:S(2)}) collective-permute-start(bf16[832,256]{1,0:T(8,128)(2,1)} %get-tuple-element.13), channel_id=1, source_target_pairs={{0,2},{1,3},{2,0},{3,1},{4,6},{5,7},{6,4},{7,5},{8,10},{9,11},{10,... | collective-permute-start | bytes 1277960 | tf_op jit(solution)/shard_map/ppermute | solution.py:397
  41.4 4.0 %collective-permute-start.2 = (bf16[832,256]{1,0:T(8,128)(2,1)}, bf16[832,256]{1,0:T(8,128)(2,1)}, u32[]{:S(2)}, u32[]{:S(2)}) collective-permute-start(bf16[832,256]{1,0:T(8,128)(2,1)} %get-tuple-element.14), channel_id=1, source_target_pairs={{0,3},{1,0},{2,1},{3,2},{4,7},{5,4},{6,5},{7,6},{8,11},{9,8},{10,9... | collective-permute-start | bytes 1277960 | tf_op jit(solution)/shard_map/ppermute | solution.py:397
  45.4 0.0 copy-done.22
  45.4 0.5 fusion.1
  45.9 1.3 %copy.16.at_ref = s32[128,1]{1,0:T(8,128)} copy(s32[128,1]{0,1:T(1,128)} %fusion.1) | data formatting | bytes 1024 | tf_op jit(solution)/shard_map/reshape | solution.py:413
  47.2 1.8 %collective-permute-done.rest_0_ = bf16[832,256]{1,0:T(8,128)(2,1)S(1)} collective-permute-done((bf16[832,256]{1,0:T(8,128)(2,1)}, bf16[832,256]{1,0:T(8,128)(2,1)S(1)}, u32[]{:S(2)}, u32[]{:S(2)}) %collective-permute-start) | collective-permute-done | bytes 426016 | tf_op jit(solution)/shard_map/ppermute | solution.py:397
  49.0 0.0 copy-start.4
  49.0 0.8 copy-done.4
  49.8 3.5 %collective-permute-done.1.rest_1_ = bf16[832,256]{1,0:T(8,128)(2,1)S(1)} collective-permute-done((bf16[832,256]{1,0:T(8,128)(2,1)}, bf16[832,256]{1,0:T(8,128)(2,1)S(1)}, u32[]{:S(2)}, u32[]{:S(2)}) %collective-permute-start.1) | collective-permute-done | bytes 426016 | tf_op jit(solution)/shard_map/ppermute | solution.py:397
  53.3 0.0 copy-start.6
  53.3 0.8 copy-done.6
  54.1 9.3 %collective-permute-done.2.rest_2_ = bf16[832,256]{1,0:T(8,128)(2,1)} collective-permute-done((bf16[832,256]{1,0:T(8,128)(2,1)}, bf16[832,256]{1,0:T(8,128)(2,1)}, u32[]{:S(2)}, u32[]{:S(2)}) %collective-permute-start.2) | collective-permute-done | bytes 426016 | tf_op jit(solution)/shard_map/ppermute | solution.py:397
  63.4 0.0 copy-done.2
  63.4 0.0 copy-done.16
  63.4 0.0 copy-done.18
  63.4 0.0 copy-done.19
  63.5 0.0 copy-start.5
  63.5 1.0 %copy-done.5 = bf16[832,256]{1,0:T(8,128)(2,1)S(1)} copy-done((bf16[832,256]{1,0:T(8,128)(2,1)S(1)}, bf16[832,256]{1,0:T(8,128)(2,1)}, u32[]{:S(2)}) %copy-start.5) | copy-done | bytes 426008
  64.5 0.0 copy-start.7
  64.5 1.0 %copy-done.7 = bf16[832,256]{1,0:T(8,128)(2,1)S(1)} copy-done((bf16[832,256]{1,0:T(8,128)(2,1)S(1)}, bf16[832,256]{1,0:T(8,128)(2,1)}, u32[]{:S(2)}) %copy-start.7) | copy-done | bytes 426008
  65.5 0.0 copy-start.13
  65.5 0.8 copy-done.13
  66.2 0.0 copy-start.14
  66.2 0.9 copy-done.14
  67.1 0.0 copy-start.9
  67.1 8.6 %before_halo.1 = (f32[2560,256]{1,0:T(8,128)}, f32[2560,256]{1,0:T(8,128)}, bf16[256,256]{1,0:T(8,128)(2,1)S(1)}, bf16[256,256]{1,0:T(8,128)(2,1)S(1)}) custom-call(s32[1]{0:T(128)} %bitcast.6.group_ref, s32[20]{0:T(128)S(1)} %copy-done.18, bf16[2560,256]{1,0:T(8,128)(2,1)S(1)} %copy-done.1, bf16[128,256]{1,0:T(8,128)(2,1)S(1)} %copy-done.8, ...), custom_call_target="tpu_custom_call" | custom-call | tf_op jit(solution)/shard_map/before_halo/pallas_call | solution.py:266
  75.7 0.6 copy-done.10
  76.4 0.0 all-to-all-done.1.halo_ref
  76.4 0.0 copy-done.3
  76.4 0.0 copy-done.9
  76.4 0.0 copy-start.11
  76.4 0.9 %copy-done.11 = bf16[256,256]{1,0:T(8,128)(2,1)S(1)} copy-done((bf16[256,256]{1,0:T(8,128)(2,1)S(1)}, bf16[256,256]{1,0:T(8,128)(2,1)}, u32[]{:S(2)}) %copy-start.11) | copy-done | bytes 131096
  77.3 0.7 copy-done.20
  78.0 0.7 copy-done.23
  78.6 10.7 %after_halo.1 = bf16[2560,256]{1,0:T(8,128)(2,1)} custom-call(s32[20]{0:T(128)S(1)} %copy-done.23, bf16[128,40,128]{2,1,0:T(8,128)(2,1)} %all-to-all-done.1.halo_ref, s32[128,1]{1,0:T(8,128)S(1)} %copy-done.9, f32[2560,256]{1,0:T(8,128)} %get-tuple-element.15.local_ref, f32[2560,256]{1,0:T(8,128)} %get-tuple-element.16.start_ref, ...), custom_call_target="tpu_custom_call" | custom-call | tf_op jit(solution)/shard_map/after_halo/pallas_call | solution.py:339
  (5 shorter events, 0.0 us)
Async XLA Ops:
  0.0 7.8 %copy-start.24 = (s32[128]{0:T(128)S(1)}, s32[128]{0:T(128)}, u32[]{:S(2)}) copy-start(s32[128]{0:T(128)} %param.21) | copy-start | bytes 1540
  0.0 7.8 %copy-start.15 = (s32[128,16]{0,1:T(8,128)S(1)}, s32[128,16]{0,1:T(8,128)}, u32[]{:S(2)}) copy-start(s32[128,16]{0,1:T(8,128)} %param.20) | copy-start | bytes 24580
  0.0 1.3 %copy-start = (bf16[2560,256]{1,0:T(8,128)(2,1)S(1)}, bf16[2560,256]{1,0:T(8,128)(2,1)}, u32[]{:S(2)}) copy-start(bf16[2560,256]{1,0:T(8,128)(2,1)} %emb_ref.9) | copy-start | bytes 3932164
  1.3 0.7 copy-start.17
  2.0 0.7 copy-start.21
  2.7 5.1 %copy-start.1 = (bf16[2560,256]{1,0:T(8,128)(2,1)S(1)}, bf16[2560,256]{1,0:T(8,128)(2,1)}, u32[]{:S(2)}) copy-start(bf16[2560,256]{1,0:T(8,128)(2,1)} %emb_ref.9) | copy-start | bytes 3932164
  3.5 9.5 %all-to-all-start = ((bf16[4,16,256]{2,1,0:T(8,128)(2,1)}), bf16[4,16,256]{2,1,0:T(8,128)(2,1)S(1)}, u32[]{:S(2)}, u32[]{:S(2)}) async-start(bf16[4,16,256]{2,1,0:T(8,128)(2,1)} %note.1), calls=%async_computation | async-start | bytes 65536 | tf_op jit(solution)/shard_map/all_to_all | solution.py:389
  13.8 18.9 %copy-start.8 = (bf16[128,256]{1,0:T(8,128)(2,1)S(1)}, bf16[128,256]{1,0:T(8,128)(2,1)}, u32[]{:S(2)}) copy-start(bf16[128,256]{1,0:T(8,128)(2,1)} %own_a.1) | copy-start | bytes 196612
  13.8 18.9 %copy-start.12 = (bf16[64,256]{1,0:T(8,128)(2,1)S(1)}, bf16[64,256]{1,0:T(8,128)(2,1)}, u32[]{:S(2)}) copy-start(bf16[64,256]{1,0:T(8,128)(2,1)} %own_b.1) | copy-start | bytes 98308
  13.8 62.6 %all-to-all-start.1 = ((bf16[128,40,128]{2,1,0:T(8,128)(2,1)}), bf16[128,40,128]{2,1,0:T(8,128)(2,1)}, u32[]{:S(2)}, u32[]{:S(2)}) async-start(bf16[128,40,128]{2,1,0:T(8,128)(2,1)} %add_drivers.1), calls=%async_computation.1 | async-start | bytes 2621440 | tf_op jit(solution)/shard_map/all_to_all | solution.py:392
  32.6 12.8 %copy-start.22 = (s32[128]{0:T(128)S(1)}, s32[128]{0:T(128)}, u32[]{:S(2)}) copy-start(s32[128]{0:T(128)} %param.22) | copy-start | bytes 1540
  32.6 30.8 %copy-start.2 = (bf16[20,2,128,128]{3,2,1,0:T(8,128)(2,1)S(1)}, bf16[20,2,128,128]{3,2,1,0:T(8,128)(2,1)}, u32[]{:S(2)}) copy-start(bf16[20,2,128,128]{3,2,1,0:T(8,128)(2,1)} %adj_ref.3) | copy-start | bytes 3932164
  32.6 30.8 %copy-start.16 = (bf16[16,256]{1,0:T(8,128)(2,1)S(1)}, bf16[16,256]{1,0:T(8,128)(2,1)}, u32[]{:S(2)}) copy-start(bf16[16,256]{1,0:T(8,128)(2,1)} %fw_ref.1) | copy-start | bytes 24580
  32.6 30.8 %copy-start.18 = (s32[20]{0:T(128)S(1)}, s32[20]{0:T(128)}, u32[]{:S(2)}) copy-start(s32[20]{0:T(128)} %slot_ref.2) | copy-start | bytes 244
  32.6 30.8 %copy-start.19 = (f32[256]{0:T(256)S(1)}, f32[256]{0:T(256)}, u32[]{:S(2)}) copy-start(f32[256]{0:T(256)} %param.25) | copy-start | bytes 3076
  35.8 13.3 %collective-permute-start = (bf16[832,256]{1,0:T(8,128)(2,1)}, bf16[832,256]{1,0:T(8,128)(2,1)S(1)}, u32[]{:S(2)}, u32[]{:S(2)}) collective-permute-start(bf16[832,256]{1,0:T(8,128)(2,1)} %get-tuple-element.12), channel_id=1, source_target_pairs={{0,1},{1,2},{2,3},{3,0},{4,5},{5,6},{6,7},{7,4},{8,9},{9,10},{10,1... | collective-permute-start | bytes 1277960 | tf_op jit(solution)/shard_map/ppermute | solution.py:397
  38.9 14.5 %collective-permute-start.1 = (bf16[832,256]{1,0:T(8,128)(2,1)}, bf16[832,256]{1,0:T(8,128)(2,1)S(1)}, u32[]{:S(2)}, u32[]{:S(2)}) collective-permute-start(bf16[832,256]{1,0:T(8,128)(2,1)} %get-tuple-element.13), channel_id=1, source_target_pairs={{0,2},{1,3},{2,0},{3,1},{4,6},{5,7},{6,4},{7,5},{8,10},{9,11},{10,... | collective-permute-start | bytes 1277960 | tf_op jit(solution)/shard_map/ppermute | solution.py:397
  41.4 22.0 %collective-permute-start.2 = (bf16[832,256]{1,0:T(8,128)(2,1)}, bf16[832,256]{1,0:T(8,128)(2,1)}, u32[]{:S(2)}, u32[]{:S(2)}) collective-permute-start(bf16[832,256]{1,0:T(8,128)(2,1)} %get-tuple-element.14), channel_id=1, source_target_pairs={{0,3},{1,0},{2,1},{3,2},{4,7},{5,4},{6,5},{7,6},{8,11},{9,8},{10,9... | collective-permute-start | bytes 1277960 | tf_op jit(solution)/shard_map/ppermute | solution.py:397
  49.0 0.8 copy-start.4
  53.3 0.8 copy-start.6
  63.5 1.0 %copy-start.5 = (bf16[832,256]{1,0:T(8,128)(2,1)S(1)}, bf16[832,256]{1,0:T(8,128)(2,1)}, u32[]{:S(2)}) copy-start(bf16[832,256]{1,0:T(8,128)(2,1)} %copy-done.4) | copy-start | bytes 1277956
  64.5 1.0 %copy-start.7 = (bf16[832,256]{1,0:T(8,128)(2,1)S(1)}, bf16[832,256]{1,0:T(8,128)(2,1)}, u32[]{:S(2)}) copy-start(bf16[832,256]{1,0:T(8,128)(2,1)} %copy-done.6) | copy-start | bytes 1277956
  65.5 0.8 copy-start.13
  66.2 0.9 copy-start.14
  67.1 9.3 %copy-start.3 = (bf16[2560,128]{1,0:T(8,128)(2,1)S(1)}, bf16[2560,128]{1,0:T(8,128)(2,1)}, u32[]{:S(2)}) copy-start(bf16[2560,128]{1,0:T(8,128)(2,1)} %dw_ref.1) | copy-start | bytes 1966084
  67.1 9.3 %copy-start.9 = (s32[128,1]{1,0:T(8,128)S(1)}, s32[128,1]{1,0:T(8,128)}, u32[]{:S(2)}) copy-start(s32[128,1]{1,0:T(8,128)} %copy.16.at_ref) | copy-start | bytes 1540
  75.7 0.6 copy-start.10
  76.4 0.9 %copy-start.11 = (bf16[256,256]{1,0:T(8,128)(2,1)S(1)}, bf16[256,256]{1,0:T(8,128)(2,1)}, u32[]{:S(2)}) copy-start(bf16[256,256]{1,0:T(8,128)(2,1)} %copy-done.10) | copy-start | bytes 393220
  77.3 0.7 copy-start.20
  78.0 0.7 copy-start.23

commit v2 on v1

v2 whole, which is shorter than its diff:
```python
import jax
import jax.numpy as jnp
from jax import lax
from jax.experimental import pallas as pl
from jax.experimental.pallas import tpu as pltpu
from jax.sharding import PartitionSpec as P

BF16, F32, I32 = jnp.bfloat16, jnp.float32, jnp.int32
NOTE = 16


def _params(mebibytes):
    return pltpu.CompilerParams(vmem_limit_bytes=mebibytes * 1024 * 1024)


def _near(x):
    return pltpu.with_memory_space_constraint(x, pltpu.VMEM)


def _far(x):
    return pltpu.with_memory_space_constraint(x, pltpu.HBM)


def _dot(a, b):
    return jnp.dot(a, b, preferred_element_type=F32)


def note(myself, hot_ids, local_slot, embedding, groups):
    rows, width = embedding.shape
    hots, tiles = hot_ids.shape[0], local_slot.shape[0]

    def body(myself_ref, hot_hbm, slot_hbm, emb_ref, out_ref, hot_ref, slot_ref, block, page, sems):
        hot_copy = pltpu.make_async_copy(hot_hbm, hot_ref, sems.at[0])
        slot_copy = pltpu.make_async_copy(slot_hbm, slot_ref, sems.at[1])
        hot_copy.start()
        slot_copy.start()
        page[...] = jnp.zeros((NOTE, width), F32)
        hot_copy.wait()
        within = hot_ref[...] - myself_ref[0] * rows
        row = jnp.max(jnp.where((within >= 0) & (within < rows), within, -1))
        start = pl.multiple_of((jnp.maximum(row, 0) // NOTE) * NOTE, NOTE)
        copy = pltpu.make_async_copy(emb_ref.at[pl.ds(start, NOTE), :], block, sems.at[2])
        copy.start()
        slot_copy.wait()
        page[1:2, :tiles] = slot_ref[...].astype(F32)
        copy.wait()
        at = lax.broadcasted_iota(I32, (NOTE, width), 0)
        mine = jnp.where(at == row - start, block[...].astype(F32), 0.0)
        page[0:1, :] = jnp.sum(mine, axis=0, keepdims=True)
        out_ref[...] = jnp.broadcast_to(page[...].astype(BF16)[None], (groups, NOTE, width))

    hbm = pl.BlockSpec(memory_space=pltpu.HBM)
    return pl.pallas_call(
        body,
        out_shape=jax.ShapeDtypeStruct((groups, NOTE, width), BF16),
        in_specs=[pl.BlockSpec(memory_space=pltpu.SMEM), hbm, hbm, hbm],
        out_specs=pl.BlockSpec((groups, NOTE, width), lambda: (0, 0, 0)),
        scratch_shapes=[
            pltpu.VMEM((1, hots), I32),
            pltpu.VMEM((1, tiles), I32),
            pltpu.VMEM((NOTE, width), BF16),
            pltpu.VMEM((NOTE, width), F32),
            pltpu.SemaphoreType.DMA((3,)),
        ],
        compiler_params=_params(1),
        name="note",
    )(myself, _far(hot_ids.reshape(1, hots)), _far(local_slot.reshape(1, tiles)), _far(embedding))


def pick_rows(send_rows, send_count, embedding):
    rows, width = embedding.shape
    doms, cap = send_rows.shape
    half = width // 2
    step = 32
    parts = rows // 128

    def body(rows_ref, count_ref, emb_ref, out_hbm, out_ref, sems):
        slot = lax.broadcasted_iota(I32, (cap, doms), 0)
        index = jnp.where(slot < count_ref[...], rows_ref[...], -1)
        low = (index & 127).astype(F32)
        high = (index >> 7).astype(F32)
        lane = lax.broadcasted_iota(I32, (cap, 128), 1).astype(F32).astype(BF16)
        one, zero = jnp.ones((), BF16), jnp.zeros((), BF16)
        copies = []
        for i in range(0, doms, step):
            chosen = []
            for p in range(i, i + step):
                low_p = jnp.broadcast_to(low[:, p : p + 1], (cap, 128)).astype(BF16)
                high_p = jnp.broadcast_to(high[:, p : p + 1], (cap, 128)).astype(BF16)
                at = jnp.where(low_p == lane, one, zero)
                chosen.append(
                    jnp.concatenate([jnp.where(high_p == jnp.asarray(k, BF16), at, zero) for k in range(parts)], axis=1)
                )
            got = _dot(jnp.concatenate(chosen, axis=0), emb_ref[...]).astype(BF16).reshape(step, cap, width)
            out_ref[i : i + step, :cap, :] = got[:, :, :half]
            out_ref[i : i + step, cap : 2 * cap, :] = got[:, :, half:]
            copies.append(
                pltpu.make_async_copy(
                    out_ref.at[i : i + step], out_hbm.at[i : i + step, : 2 * cap, :], sems.at[i // step]
                )
            )
            copies[-1].start()
        for copy in copies:
            copy.wait()

    return pl.pallas_call(
        body,
        out_shape=pltpu.HBM((doms, 2 * cap + 8, half), BF16),
        in_specs=[
            pl.BlockSpec((cap, doms), lambda: (0, 0)),
            pl.BlockSpec((1, doms), lambda: (0, 0)),
            pl.BlockSpec((rows, width), lambda: (0, 0)),
        ],
        out_specs=pl.BlockSpec(memory_space=pl.ANY),
        scratch_shapes=[pltpu.VMEM((doms, 2 * cap, half), BF16), pltpu.SemaphoreType.DMA((doms // step,))],
        compiler_params=_params(24),
        name="pick_rows",
    )(_near(send_rows.T), _near(send_count.reshape(1, doms)), _near(embedding))


def add_drivers(notes, message):
    doms, length, half = message.shape
    groups = notes.shape[0]

    def body(notes_ref, _, out_ref, page, sem):
        at = lax.broadcasted_iota(I32, (8, half), 0)
        last = jnp.zeros((8, half), F32)
        for g in range(groups):
            row = notes_ref[g].astype(F32)[0:1, :]
            last = jnp.where(at == g, row[:, :half], last)
            last = jnp.where(at == groups + g, row[:, half:], last)
        page[...] = jnp.broadcast_to(last[None], (doms, 8, half)).astype(BF16)
        copy = pltpu.make_async_copy(page, out_ref.at[:, pl.ds(length - 8, 8), :], sem)
        copy.start()
        copy.wait()

    return pl.pallas_call(
        body,
        out_shape=jax.ShapeDtypeStruct(message.shape, BF16),
        in_specs=[pl.BlockSpec(notes.shape, lambda: (0, 0, 0)), pl.BlockSpec(memory_space=pl.ANY)],
        out_specs=pl.BlockSpec(memory_space=pl.ANY),
        scratch_shapes=[pltpu.VMEM((doms, 8, half), BF16), pltpu.SemaphoreType.DMA(())],
        input_output_aliases={1: 0},
        compiler_params=_params(2),
        name="add_drivers",
    )(notes, _far(message))


def pick_tiles(group, slots, embedding, first_weight, second_weight, tile):
    groups, tiles = slots.shape
    rows, width = embedding.shape
    each = tiles // groups
    a, b = first_weight.shape[0], second_weight.shape[0]
    length = each * tile + a + b

    def body(group_ref, slots_ref, emb_ref, first_ref, second_ref, *rest):
        outs, (listed, sems) = rest[: groups - 1], rest[groups - 1 :]
        me = group_ref[0]
        copies = []
        for k in range(1, groups):
            out = outs[k - 1]
            other = (me + k) % groups
            copies.append(pltpu.make_async_copy(first_ref, out.at[pl.ds(each * tile, a), :], sems.at[k - 1, each]))
            copies.append(
                pltpu.make_async_copy(second_ref, out.at[pl.ds(each * tile + a, b), :], sems.at[k - 1, each + 1])
            )
            for j in range(each):
                listed[k - 1, j] = 0

            def look(t, found, k=k, other=other):
                tile_at = slots_ref[other, t]
                hit = tile_at // tiles == me

                @pl.when(hit)
                def _():
                    listed[k - 1, jnp.minimum(found, each - 1)] = tile_at - me * tiles

                return found + hit.astype(I32)

            lax.fori_loop(0, tiles, look, jnp.zeros((), I32))
            for j in range(each):
                start = pl.multiple_of(listed[k - 1, j] * tile, tile)
                copies.append(
                    pltpu.make_async_copy(
                        emb_ref.at[pl.ds(start, tile), :], out.at[pl.ds(j * tile, tile), :], sems.at[k - 1, j]
                    )
                )
        for copy in copies:
            copy.start()
        for copy in copies:
            copy.wait()

    hbm = pl.BlockSpec(memory_space=pl.ANY)
    smem = pl.BlockSpec(memory_space=pltpu.SMEM)
    return pl.pallas_call(
        body,
        out_shape=[pltpu.HBM((length, width), BF16)] * (groups - 1),
        in_specs=[smem, smem, hbm, hbm, hbm],
        out_specs=[hbm] * (groups - 1),
        scratch_shapes=[
            pltpu.SMEM((groups - 1, each), I32),
            pltpu.SemaphoreType.DMA((groups - 1, each + 2)),
        ],
        compiler_params=_params(2),
        name="pick_tiles",
    )(group, slots, _near(embedding), first_weight, second_weight)


def ready(
    group, slot, embedding, arrived, first_weight, second_weight, feats, feature_weight, first_bias, tile
):
    rows, width = embedding.shape
    tiles = slot.shape[0]
    groups = len(arrived) + 1
    each = tiles // groups
    a, b = first_weight.shape[0], second_weight.shape[0]
    many = rows // 4

    def body(group_ref, slot_ref, emb_ref, own_a, own_b, feat_hbm, fw_hbm, bias_hbm, *rest):
        parts = rest[: groups - 1]
        tiles_ref, start_hbm, lower_ref, second_ref, *rest = rest[groups - 1 :]
        start_ref, weight, feat_ref, fw_ref, bias_ref, tile_sems, start_sems, sems, small_sems = rest
        me = group_ref[0]
        small = [
            pltpu.make_async_copy(feat_hbm, feat_ref, small_sems.at[0]),
            pltpu.make_async_copy(fw_hbm, fw_ref, small_sems.at[1]),
            pltpu.make_async_copy(bias_hbm, bias_ref, small_sems.at[2]),
        ]
        firsts, seconds = [], []
        for k in range(groups):
            other = (me + groups - k) % groups
            from_a = own_a if k == 0 else parts[k - 1].at[pl.ds(each * tile, a), :]
            from_b = own_b if k == 0 else parts[k - 1].at[pl.ds(each * tile + a, b), :]
            to_a = weight.at[pl.ds(pl.multiple_of(other * a, a), a), :]
            to_b = second_ref.at[pl.ds(pl.multiple_of(other * b, b), b), :]
            firsts.append(pltpu.make_async_copy(from_a, to_a, sems.at[0, k]))
            seconds.append(pltpu.make_async_copy(from_b, to_b, sems.at[1, k]))
        for copy in (*firsts, *small, *seconds):
            copy.start()

        def send(t, counts):
            source = slot_ref[t] // tiles
            spot = sum(jnp.where(source == g, counts[g], 0) for g in range(groups))
            away = (me + groups - source) % groups
            for k in range(groups):

                @pl.when(away == k)
                def _(k=k):
                    if k == 0:
                        at = pl.multiple_of((slot_ref[t] - source * tiles) * tile, tile)
                        copy = pltpu.make_async_copy(emb_ref.at[pl.ds(at, tile), :], tiles_ref.at[t], tile_sems.at[t])
                    else:
                        at = pl.multiple_of(jnp.minimum(spot, each - 1) * tile, tile)
                        here = parts[k - 1].at[pl.ds(at, tile), :]
                        copy = pltpu.make_async_copy(here, tiles_ref.at[t], tile_sems.at[t])
                    copy.start()

            return tuple(counts[g] + (source == g).astype(I32) for g in range(groups))

        lax.fori_loop(0, tiles, send, (jnp.zeros((), I32),) * groups)
        for copy in (*firsts, *small):
            copy.wait()
        leaving = [pltpu.make_async_copy(weight.at[pl.ds(width, width), :], lower_ref, small_sems.at[0])]
        leaving[0].start()
        for n in range(rows // many):
            here = pl.ds(n * many, many)
            start_ref[here, :] = (
                _dot(emb_ref[here, :], weight[:width, :])
                + lax.dot_general(
                    feat_ref[:, n * many : (n + 1) * many],
                    fw_ref[...],
                    (((0,), (0,)), ((), ())),
                    preferred_element_type=F32,
                )
                + bias_ref[...]
            )
            leaving.append(pltpu.make_async_copy(start_ref.at[here, :], start_hbm.at[here, :], start_sems.at[n]))
            leaving[-1].start()
        for copy in (*seconds, *leaving):
            copy.wait()
        for t in range(tiles):
            pltpu.make_async_copy(emb_ref.at[pl.ds(0, tile), :], tiles_ref.at[t], tile_sems.at[t]).wait()

    smem = pl.BlockSpec(memory_space=pltpu.SMEM)
    hbm = pl.BlockSpec(memory_space=pltpu.HBM)
    return pl.pallas_call(
        body,
        out_shape=[
            pltpu.HBM((tiles, tile, width), BF16),
            pltpu.HBM((rows, width), F32),
            pltpu.HBM((width, width), BF16),
            pltpu.HBM((width, width), BF16),
        ],
        in_specs=[smem, smem, pl.BlockSpec(memory_space=pltpu.VMEM)] + [hbm] * (5 + len(arrived)),
        out_specs=[hbm] * 4,
        scratch_shapes=[
            pltpu.VMEM((rows, width), F32),
            pltpu.VMEM((2 * width, width), BF16),
            pltpu.VMEM(feats.shape, BF16),
            pltpu.VMEM(feature_weight.shape, BF16),
            pltpu.VMEM(first_bias.shape, F32),
            pltpu.SemaphoreType.DMA((tiles,)),
            pltpu.SemaphoreType.DMA((rows // many,)),
            pltpu.SemaphoreType.DMA((2, groups)),
            pltpu.SemaphoreType.DMA((3,)),
        ],
        compiler_params=_params(12),
        name="ready",
    )(
        group,
        slot,
        _near(embedding),
        *map(_far, (first_weight, second_weight, feats, feature_weight, first_bias, *arrived)),
    )


def after_halo(
    halo_slot, halo, driver_at, local_tiles, start, adjacency, driver_weight, embedding, lower, second, second_bias
):
    rows, width = embedding.shape
    tiles, _, tile, _ = adjacency.shape
    doms, length, half = halo.shape
    cap = (length - 8) // 2
    hots = driver_weight.shape[1]
    many = tiles // 4
    block = many * tile
    per = tile // cap

    def body(
        halo_hbm, local_hbm, start_hbm, lower_hbm, second_hbm, slot_hbm, bias_hbm, at_ref, adj_ref, dw_ref, emb_ref,
        out_hbm, halo_ref, local_ref, start_ref, lower_ref, second_ref, slot_ref, bias_ref, out, sems, in_sems, out_sems,
    ):
        halo_copy = pltpu.make_async_copy(halo_hbm, halo_ref, sems.at[0])
        slot_copy = pltpu.make_async_copy(slot_hbm, slot_ref, sems.at[1])
        rest = [
            pltpu.make_async_copy(lower_hbm, lower_ref, sems.at[2]),
            pltpu.make_async_copy(second_hbm, second_ref, sems.at[3]),
            pltpu.make_async_copy(bias_hbm, bias_ref, sems.at[4]),
        ]
        blocks = tiles // many
        locals_, starts = [], []
        for n in range(blocks):
            these, here = pl.ds(n * many, many), pl.ds(n * block, block)
            locals_.append(pltpu.make_async_copy(local_hbm.at[these], local_ref.at[these], in_sems.at[0, n]))
            starts.append(pltpu.make_async_copy(start_hbm.at[here, :], start_ref.at[here, :], in_sems.at[1, n]))
        slot_copy.start()
        halo_copy.start()
        for n in range(blocks):
            locals_[n].start()
            if n == 0:
                for copy in rest:
                    copy.start()
            starts[n].start()
        halo_copy.wait()
        column = lax.broadcasted_iota(I32, (hots, doms * 8), 1)
        ends = halo_ref[:, 2 * cap :, :].reshape(doms * 8, half)
        left = jnp.where(column == at_ref[...], 1.0, 0.0).astype(BF16)
        right = jnp.where(column == at_ref[...] + 4, 1.0, 0.0).astype(BF16)
        drivers = jnp.concatenate([_dot(left, ends).astype(BF16), _dot(right, ends).astype(BF16)], axis=1)
        slot_copy.wait()
        copies = []
        for n in range(blocks):
            locals_[n].wait()
            if n == 0:
                for copy in rest:
                    copy.wait()
            starts[n].wait()
            aggregate = []
            for t in range(n * many, (n + 1) * many):
                which = pl.ds(pl.multiple_of(slot_ref[0, t] * per, per), per)
                halo_tile = jnp.concatenate(
                    [
                        halo_ref[which, :cap, :].reshape(tile, half),
                        halo_ref[which, cap : 2 * cap, :].reshape(tile, half),
                    ],
                    axis=1,
                )
                edges = jnp.concatenate([adj_ref[t, 0], adj_ref[t, 1], dw_ref[t * tile : (t + 1) * tile, :]], axis=1)
                sources = jnp.concatenate([local_ref[t], halo_tile, drivers], axis=0)
                aggregate.append(_dot(edges, sources).astype(BF16))
            here = slice(n * block, (n + 1) * block)
            inner = start_ref[here, :] + _dot(jnp.concatenate(aggregate, axis=0), lower_ref[...])
            activated = (0.5 * inner * (1.0 + lax.erf(inner * (0.5**0.5)))).astype(BF16)
            out[here, :] = (emb_ref[here, :].astype(F32) + bias_ref[...] + _dot(activated, second_ref[...])).astype(
                BF16
            )
            copies.append(pltpu.make_async_copy(out.at[here, :], out_hbm.at[here, :], out_sems.at[n]))
            copies[-1].start()
        for copy in copies:
            copy.wait()

    hbm = pl.BlockSpec(memory_space=pltpu.HBM)
    vmem = pl.BlockSpec(memory_space=pltpu.VMEM)
    return pl.pallas_call(
        body,
        out_shape=jax.ShapeDtypeStruct((rows, width), BF16),
        in_specs=[hbm] * 7 + [vmem] * 4,
        out_specs=hbm,
        scratch_shapes=[
            pltpu.VMEM(halo.shape, BF16),
            pltpu.VMEM(local_tiles.shape, BF16),
            pltpu.VMEM(start.shape, F32),
            pltpu.VMEM(lower.shape, BF16),
            pltpu.VMEM(second.shape, BF16),
            pltpu.SMEM((1, tiles), I32),
            pltpu.VMEM(second_bias.shape, F32),
            pltpu.VMEM((rows, width), BF16),
            pltpu.SemaphoreType.DMA((5,)),
            pltpu.SemaphoreType.DMA((2, tiles // many)),
            pltpu.SemaphoreType.DMA((tiles // many,)),
        ],
        compiler_params=_params(24),
        name="after_halo",
    )(
        *map(_far, (halo, local_tiles, start, lower, second, halo_slot.reshape(1, tiles), second_bias)),
        *map(_near, (driver_at, adjacency, driver_weight, embedding)),
    )


def per_device(
    embedding,
    scenario_feats,
    adjacency,
    driver_weight,
    local_slot,
    halo_slot,
    send_rows,
    send_count,
    hot_ids,
    first_weight,
    feature_weight,
    first_bias,
    second_weight,
    second_bias,
):
    rows, width = embedding.shape
    tile = adjacency.shape[-1]
    tiles = rows // tile
    groups = lax.axis_size("scen")
    myself = lax.axis_index(("dom", "scen")).astype(I32).reshape(1)
    group = lax.axis_index("scen").astype(I32).reshape(1)

    page = note(myself, hot_ids, local_slot, embedding, groups)
    notes = lax.all_to_all(page, "scen", split_axis=0, concat_axis=0, tiled=True)
    message = pick_rows(send_rows, send_count, embedding)
    message = add_drivers(notes, message)
    halo = lax.all_to_all(message, "dom", split_axis=0, concat_axis=0, tiled=True)

    slots = notes[:, 1, :tiles].astype(I32)
    leaving = pick_tiles(group, slots, embedding, first_weight, second_weight, tile)
    arrived = [
        lax.ppermute(x, "scen", [(g, (g + k) % groups) for g in range(groups)])
        for k, x in enumerate(leaving, start=1)
    ]
    local_tiles, start, lower, second = ready(
        group,
        local_slot,
        embedding,
        arrived,
        first_weight,
        second_weight,
        scenario_feats,
        feature_weight,
        first_bias.reshape(1, width),
        tile,
    )
    owner = hot_ids // rows
    driver_at = (owner // groups * 8 + owner % groups).reshape(-1, 1)
    return after_halo(
        halo_slot,
        halo,
        driver_at,
        local_tiles,
        start,
        adjacency,
        driver_weight,
        embedding,
        lower,
        second,
        second_bias.reshape(1, width),
    )


def solution(mesh):
    return jax.shard_map(
        per_device,
        mesh=mesh,
        in_specs=(
            P(("dom", "scen"), None),
            P(None, ("dom", "scen")),
            P(("dom", "scen"), None, None, None),
            P(("dom", "scen"), None),
            P(("dom", "scen")),
            P(("dom", "scen")),
            P(("dom", "scen"), None),
            P(("dom", "scen")),
            P(),
            P("scen", None),
            P(),
            P(),
            P("scen", None),
            P(),
        ),
        out_specs=P(("dom", "scen"), None),
        check_vma=False,
    )
```

time: 90.2 us -> 104 us (1.15)
  the two profiles are of different devices: /device:TPU:19 before, /device:TPU:15 now
where the time goes in v2:
time: 104 us; the launch traced here: 103 us
  Pallas kernels  51.3 us (49%)
  starting transfers between devices  31.1 us (30%)
  waiting for transfers between devices  19.5 us (19%)
    pallas_call x1, Pallas kernels, ready(): pl.pallas_call(body, out_shape=[pltpu.HBM((tiles, tile, width), BF16), pl...  35.7 us
    ppermute x3, waiting for transfers between devices, per_device(): lax.ppermute(x, 'scen', [(g, (g + k) % groups) for g in range(groups)])  19.5 us
    all_to_all x1, starting transfers between devices, per_device(): lax.all_to_all(message, 'dom', split_axis=0, concat_axis=0, tiled=True)  18.8 us
    ppermute x3, starting transfers between devices, per_device(): lax.ppermute(x, 'scen', [(g, (g + k) % groups) for g in range(groups)])  8.1 us
    pallas_call x1, Pallas kernels, after_halo(): pl.pallas_call(body, out_shape=jax.ShapeDtypeStruct((rows, width), BF16),...  5.71 us
    all_to_all x1, starting transfers between devices, per_device(): lax.all_to_all(page, 'scen', split_axis=0, concat_axis=0, tiled=True)  4.22 us
    pallas_call x1, Pallas kernels, pick_rows(): pl.pallas_call(body, out_shape=pltpu.HBM((doms, 2 * cap + 8, half), BF16)...  3.83 us
    pallas_call x1, Pallas kernels, pick_tiles(): pl.pallas_call(body, out_shape=[pltpu.HBM((length, width), BF16)] * (grou...  3.03 us
  transfers between devices with their start and end apart: 5, of which 3 were waited for; matrix products, arithmetic and copies ran while one was open for 0% of the time, Pallas kernels for 41%

profile of v2, /device:TPU:15, one launch (start us, length us, event | category | flops | bytes accessed | tf_op | source)
XLA Modules:
  0.0 103.2 jit_solution(1051896841930115558)
XLA Ops:
  0.0 0.0 copy-start
  0.0 0.0 copy-start.7
  0.0 0.0 copy-start.5
  0.0 2.3 %note.1 = bf16[4,16,256]{2,1,0:T(8,128)(2,1)} custom-call(s32[1]{0:T(128)} %bitcast.myself_ref, s32[1,128]{1,0:T(1,128)} %bitcast.18, s32[1,20]{1,0:T(1,128)} %bitcast.14, bf16[2560,256]{1,0:T(8,128)(2,1)} %emb_ref.9), custom_call_target="tpu_custom_call" | custom-call | tf_op jit(solution)/shard_map/note/pallas_call | solution.py:53
  2.3 4.2 %all-to-all-start = ((bf16[4,16,256]{2,1,0:T(8,128)(2,1)}), bf16[4,16,256]{2,1,0:T(8,128)(2,1)S(1)}, u32[]{:S(2)}, u32[]{:S(2)}) async-start(bf16[4,16,256]{2,1,0:T(8,128)(2,1)} %note.1), calls=%async_computation | async-start | bytes 65536 | tf_op jit(solution)/shard_map/all_to_all | solution.py:444
  6.6 0.0 copy-done
  6.6 0.0 copy-done.7
  6.6 0.0 copy-done.5
  6.6 3.8 %pick_rows.1._ = bf16[128,40,128]{2,1,0:T(8,128)(2,1)} custom-call(s32[16,128]{1,0:T(8,128)S(1)} %bitcast.12, s32[1,128]{1,0:T(1,128)S(1)} %bitcast.15, bf16[2560,256]{1,0:T(8,128)(2,1)S(1)} %copy-done), custom_call_target="tpu_custom_call" | custom-call | tf_op jit(solution)/shard_map/pick_rows/pallas_call | solution.py:106
  10.4 0.0 all-to-all-done.notes_ref
  10.4 0.7 add_drivers.1
  11.2 0.0 copy-start.3
  11.2 0.0 copy-start.4
  11.2 18.8 %all-to-all-start.1 = ((bf16[128,40,128]{2,1,0:T(8,128)(2,1)}), bf16[128,40,128]{2,1,0:T(8,128)(2,1)}, u32[]{:S(2)}, u32[]{:S(2)}) async-start(bf16[128,40,128]{2,1,0:T(8,128)(2,1)} %add_drivers.1), calls=%async_computation.1 | async-start | bytes 2621440 | tf_op jit(solution)/shard_map/all_to_all | solution.py:447
  30.0 0.0 copy-start.11
  30.0 0.0 copy-start.6
  30.0 0.0 copy-done.3
  30.0 0.0 copy-done.4
  30.1 3.0 %pick_tiles.1 = (bf16[832,256]{1,0:T(8,128)(2,1)}, bf16[832,256]{1,0:T(8,128)(2,1)}, bf16[832,256]{1,0:T(8,128)(2,1)}) custom-call(s32[1]{0:T(128)} %bitcast.5.group_ref, s32[4,20]{1,0:T(4,128)S(1)} %bitcast.13, bf16[2560,256]{1,0:T(8,128)(2,1)S(1)} %copy-done, bf16[128,256]{1,0:T(8,128)(2,1)S(1)} %copy-done.3, bf16[64,256]{1,0:T(8,128)(2,1)S(1)} %copy-done.4), custom_call_target="tpu_custom_call" | custom-call | tf_op jit(solution)/shard_map/pick_tiles/pallas_call | solution.py:195
  33.1 3.2 %collective-permute-start = (bf16[832,256]{1,0:T(8,128)(2,1)}, bf16[832,256]{1,0:T(8,128)(2,1)S(1)}, u32[]{:S(2)}, u32[]{:S(2)}) collective-permute-start(bf16[832,256]{1,0:T(8,128)(2,1)} %get-tuple-element.12), channel_id=1, source_target_pairs={{0,1},{1,2},{2,3},{3,0},{4,5},{5,6},{6,7},{7,4},{8,9},{9,10},{10,1... | collective-permute-start | bytes 1277960 | tf_op jit(solution)/shard_map/ppermute | solution.py:452
  36.3 3.0 %collective-permute-start.1 = (bf16[832,256]{1,0:T(8,128)(2,1)}, bf16[832,256]{1,0:T(8,128)(2,1)S(1)}, u32[]{:S(2)}, u32[]{:S(2)}) collective-permute-start(bf16[832,256]{1,0:T(8,128)(2,1)} %get-tuple-element.13), channel_id=1, source_target_pairs={{0,2},{1,3},{2,0},{3,1},{4,6},{5,7},{6,4},{7,5},{8,10},{9,11},{10,... | collective-permute-start | bytes 1277960 | tf_op jit(solution)/shard_map/ppermute | solution.py:452
  39.3 1.9 %collective-permute-start.2 = (bf16[832,256]{1,0:T(8,128)(2,1)}, bf16[832,256]{1,0:T(8,128)(2,1)S(1)}, u32[]{:S(2)}, u32[]{:S(2)}) collective-permute-start(bf16[832,256]{1,0:T(8,128)(2,1)} %get-tuple-element.14), channel_id=1, source_target_pairs={{0,3},{1,0},{2,1},{3,2},{4,7},{5,4},{6,5},{7,6},{8,11},{9,8},{10,9... | collective-permute-start | bytes 1277960 | tf_op jit(solution)/shard_map/ppermute | solution.py:452
  41.2 0.0 copy-done.11
  41.2 0.1 copy.16.at_ref
  41.4 5.0 %collective-permute-done.rest_0_ = bf16[832,256]{1,0:T(8,128)(2,1)S(1)} collective-permute-done((bf16[832,256]{1,0:T(8,128)(2,1)}, bf16[832,256]{1,0:T(8,128)(2,1)S(1)}, u32[]{:S(2)}, u32[]{:S(2)}) %collective-permute-start) | collective-permute-done | bytes 426016 | tf_op jit(solution)/shard_map/ppermute | solution.py:452
  46.3 0.0 copy-start.8
  46.3 4.5 %collective-permute-done.1.rest_1_ = bf16[832,256]{1,0:T(8,128)(2,1)S(1)} collective-permute-done((bf16[832,256]{1,0:T(8,128)(2,1)}, bf16[832,256]{1,0:T(8,128)(2,1)S(1)}, u32[]{:S(2)}, u32[]{:S(2)}) %collective-permute-start.1) | collective-permute-done | bytes 426016 | tf_op jit(solution)/shard_map/ppermute | solution.py:452
  50.8 0.0 copy-start.9
  50.8 10.1 %collective-permute-done.2.rest_2_ = bf16[832,256]{1,0:T(8,128)(2,1)S(1)} collective-permute-done((bf16[832,256]{1,0:T(8,128)(2,1)}, bf16[832,256]{1,0:T(8,128)(2,1)S(1)}, u32[]{:S(2)}, u32[]{:S(2)}) %collective-permute-start.2) | collective-permute-done | bytes 426016 | tf_op jit(solution)/shard_map/ppermute | solution.py:452
  60.9 0.0 copy-done.8
  60.9 0.0 copy-done.9
  60.9 0.0 copy-start.10
  60.9 0.8 copy-done.10
  61.7 0.0 copy-done.6
  61.7 0.0 copy-start.1
  61.7 0.0 copy-start.2
  61.7 35.7 %ready.1 = (bf16[20,128,256]{2,1,0:T(8,128)(2,1)}, f32[2560,256]{1,0:T(8,128)}, bf16[256,256]{1,0:T(8,128)(2,1)}, bf16[256,256]{1,0:T(8,128)(2,1)}) custom-call(s32[1]{0:T(128)} %bitcast.5.group_ref, s32[20]{0:T(128)S(1)} %copy-done.6, bf16[2560,256]{1,0:T(8,128)(2,1)S(1)} %copy-done, bf16[128,256]{1,0:T(8,128)(2,1)} %own_a.1, bf16[64,256]{1,0:T(8,128)(2,1)} %own_b.1, ...), custom_call_target="tpu_custom_call" | custom-call | tf_op jit(solution)/shard_map/ready/pallas_call | solution.py:286
  97.4 0.0 all-to-all-done.1.halo_hbm
  97.4 0.0 copy-done.1
  97.4 0.0 copy-done.2
  97.4 5.7 %after_halo.1 = bf16[2560,256]{1,0:T(8,128)(2,1)} custom-call(bf16[128,40,128]{2,1,0:T(8,128)(2,1)} %all-to-all-done.1.halo_hbm, bf16[20,128,256]{2,1,0:T(8,128)(2,1)} %get-tuple-element.15.local_hbm, f32[2560,256]{1,0:T(8,128)} %get-tuple-element.16.start_hbm, bf16[256,256]{1,0:T(8,128)(2,1)} %get-tuple-element.17.lower_hbm, ...), custom_call_target="tpu_custom_call" | custom-call | tf_op jit(solution)/shard_map/after_halo/pallas_call | solution.py:394
  (2 shorter events, 0.0 us)
Async XLA Ops:
  0.0 6.6 %copy-start = (bf16[2560,256]{1,0:T(8,128)(2,1)S(1)}, bf16[2560,256]{1,0:T(8,128)(2,1)}, u32[]{:S(2)}) copy-start(bf16[2560,256]{1,0:T(8,128)(2,1)} %emb_ref.9) | copy-start | bytes 3932164
  0.0 6.6 %copy-start.7 = (s32[128]{0:T(128)S(1)}, s32[128]{0:T(128)}, u32[]{:S(2)}) copy-start(s32[128]{0:T(128)} %param.21) | copy-start | bytes 1540
  0.0 6.6 %copy-start.5 = (s32[128,16]{0,1:T(8,128)S(1)}, s32[128,16]{0,1:T(8,128)}, u32[]{:S(2)}) copy-start(s32[128,16]{0,1:T(8,128)} %param.20) | copy-start | bytes 24580
  2.3 8.1 %all-to-all-start = ((bf16[4,16,256]{2,1,0:T(8,128)(2,1)}), bf16[4,16,256]{2,1,0:T(8,128)(2,1)S(1)}, u32[]{:S(2)}, u32[]{:S(2)}) async-start(bf16[4,16,256]{2,1,0:T(8,128)(2,1)} %note.1), calls=%async_computation | async-start | bytes 65536 | tf_op jit(solution)/shard_map/all_to_all | solution.py:444
  11.2 18.9 %copy-start.3 = (bf16[128,256]{1,0:T(8,128)(2,1)S(1)}, bf16[128,256]{1,0:T(8,128)(2,1)}, u32[]{:S(2)}) copy-start(bf16[128,256]{1,0:T(8,128)(2,1)} %own_a.1) | copy-start | bytes 196612
  11.2 18.9 %copy-start.4 = (bf16[64,256]{1,0:T(8,128)(2,1)S(1)}, bf16[64,256]{1,0:T(8,128)(2,1)}, u32[]{:S(2)}) copy-start(bf16[64,256]{1,0:T(8,128)(2,1)} %own_b.1) | copy-start | bytes 98308
  11.2 86.2 %all-to-all-start.1 = ((bf16[128,40,128]{2,1,0:T(8,128)(2,1)}), bf16[128,40,128]{2,1,0:T(8,128)(2,1)}, u32[]{:S(2)}, u32[]{:S(2)}) async-start(bf16[128,40,128]{2,1,0:T(8,128)(2,1)} %add_drivers.1), calls=%async_computation.1 | async-start | bytes 2621440 | tf_op jit(solution)/shard_map/all_to_all | solution.py:447
  30.0 11.2 %copy-start.11 = (s32[128]{0:T(128)S(1)}, s32[128]{0:T(128)}, u32[]{:S(2)}) copy-start(s32[128]{0:T(128)} %param.22) | copy-start | bytes 1540
  30.0 31.7 %copy-start.6 = (s32[20]{0:T(128)S(1)}, s32[20]{0:T(128)}, u32[]{:S(2)}) copy-start(s32[20]{0:T(128)} %slot_ref.1) | copy-start | bytes 244
  33.1 13.3 %collective-permute-start = (bf16[832,256]{1,0:T(8,128)(2,1)}, bf16[832,256]{1,0:T(8,128)(2,1)S(1)}, u32[]{:S(2)}, u32[]{:S(2)}) collective-permute-start(bf16[832,256]{1,0:T(8,128)(2,1)} %get-tuple-element.12), channel_id=1, source_target_pairs={{0,1},{1,2},{2,3},{3,0},{4,5},{5,6},{6,7},{7,4},{8,9},{9,10},{10,1... | collective-permute-start | bytes 1277960 | tf_op jit(solution)/shard_map/ppermute | solution.py:452
  36.3 14.5 %collective-permute-start.1 = (bf16[832,256]{1,0:T(8,128)(2,1)}, bf16[832,256]{1,0:T(8,128)(2,1)S(1)}, u32[]{:S(2)}, u32[]{:S(2)}) collective-permute-start(bf16[832,256]{1,0:T(8,128)(2,1)} %get-tuple-element.13), channel_id=1, source_target_pairs={{0,2},{1,3},{2,0},{3,1},{4,6},{5,7},{6,4},{7,5},{8,10},{9,11},{10,... | collective-permute-start | bytes 1277960 | tf_op jit(solution)/shard_map/ppermute | solution.py:452
  39.3 21.6 %collective-permute-start.2 = (bf16[832,256]{1,0:T(8,128)(2,1)}, bf16[832,256]{1,0:T(8,128)(2,1)S(1)}, u32[]{:S(2)}, u32[]{:S(2)}) collective-permute-start(bf16[832,256]{1,0:T(8,128)(2,1)} %get-tuple-element.14), channel_id=1, source_target_pairs={{0,3},{1,0},{2,1},{3,2},{4,7},{5,4},{6,5},{7,6},{8,11},{9,8},{10,9... | collective-permute-start | bytes 1277960 | tf_op jit(solution)/shard_map/ppermute | solution.py:452
  46.3 14.6 %copy-start.8 = (bf16[832,256]{1,0:T(8,128)(2,1)}, bf16[832,256]{1,0:T(8,128)(2,1)S(1)}, u32[]{:S(2)}) copy-start(bf16[832,256]{1,0:T(8,128)(2,1)S(1)} %collective-permute-done.rest_0_) | copy-start | bytes 1277956
  50.8 10.1 %copy-start.9 = (bf16[832,256]{1,0:T(8,128)(2,1)}, bf16[832,256]{1,0:T(8,128)(2,1)S(1)}, u32[]{:S(2)}) copy-start(bf16[832,256]{1,0:T(8,128)(2,1)S(1)} %collective-permute-done.1.rest_1_) | copy-start | bytes 1277956
  60.9 0.8 copy-start.10
  61.7 35.8 %copy-start.1 = (bf16[20,2,128,128]{3,2,1,0:T(8,128)(2,1)S(1)}, bf16[20,2,128,128]{3,2,1,0:T(8,128)(2,1)}, u32[]{:S(2)}) copy-start(bf16[20,2,128,128]{3,2,1,0:T(8,128)(2,1)} %adj_ref.1) | copy-start | bytes 3932164
  61.7 35.8 %copy-start.2 = (bf16[2560,128]{1,0:T(8,128)(2,1)S(1)}, bf16[2560,128]{1,0:T(8,128)(2,1)}, u32[]{:S(2)}) copy-start(bf16[2560,128]{1,0:T(8,128)(2,1)} %dw_ref.1) | copy-start | bytes 1966084

commit v3 on v2

--- a/solution.py
+++ b/solution.py
@@ -52,9 +52,9 @@
     hbm = pl.BlockSpec(memory_space=pltpu.HBM)
     return pl.pallas_call(
         body,
-        out_shape=jax.ShapeDtypeStruct((groups, NOTE, width), BF16),
+        out_shape=pltpu.VMEM((groups, NOTE, width), BF16),
         in_specs=[pl.BlockSpec(memory_space=pltpu.SMEM), hbm, hbm, hbm],
-        out_specs=pl.BlockSpec((groups, NOTE, width), lambda: (0, 0, 0)),
+        out_specs=pl.BlockSpec(memory_space=pltpu.VMEM),
         scratch_shapes=[
             pltpu.VMEM((1, hots), I32),
             pltpu.VMEM((1, tiles), I32),
@@ -218,8 +218,8 @@
 
     def body(group_ref, slot_ref, emb_ref, own_a, own_b, feat_hbm, fw_hbm, bias_hbm, *rest):
         parts = rest[: groups - 1]
-        tiles_ref, start_hbm, lower_ref, second_ref, *rest = rest[groups - 1 :]
-        start_ref, weight, feat_ref, fw_ref, bias_ref, tile_sems, start_sems, sems, small_sems = rest
+        tiles_hbm, start_hbm, lower_ref, second_hbm, *rest = rest[groups - 1 :]
+        tiles_ref, start_ref, weight, second_ref, feat_ref, fw_ref, bias_ref, tile_sems, start_sems, sems, small_sems = rest
         me = group_ref[0]
         small = [
             pltpu.make_async_copy(feat_hbm, feat_ref, small_sems.at[0]),
@@ -276,10 +276,16 @@
             )
             leaving.append(pltpu.make_async_copy(start_ref.at[here, :], start_hbm.at[here, :], start_sems.at[n]))
             leaving[-1].start()
-        for copy in (*seconds, *leaving):
-            copy.wait()
         for t in range(tiles):
             pltpu.make_async_copy(emb_ref.at[pl.ds(0, tile), :], tiles_ref.at[t], tile_sems.at[t]).wait()
+        leaving.append(pltpu.make_async_copy(tiles_ref, tiles_hbm, small_sems.at[1]))
+        leaving[-1].start()
+        for copy in seconds:
+            copy.wait()
+        leaving.append(pltpu.make_async_copy(second_ref, second_hbm, small_sems.at[2]))
+        leaving[-1].start()
+        for copy in leaving:
+            copy.wait()
 
     smem = pl.BlockSpec(memory_space=pltpu.SMEM)
     hbm = pl.BlockSpec(memory_space=pltpu.HBM)
@@ -294,8 +300,10 @@
         in_specs=[smem, smem, pl.BlockSpec(memory_space=pltpu.VMEM)] + [hbm] * (5 + len(arrived)),
         out_specs=[hbm] * 4,
         scratch_shapes=[
+            pltpu.VMEM((tiles, tile, width), BF16),
             pltpu.VMEM((rows, width), F32),
             pltpu.VMEM((2 * width, width), BF16),
+            pltpu.VMEM((width, width), BF16),
             pltpu.VMEM(feats.shape, BF16),
             pltpu.VMEM(feature_weight.shape, BF16),
             pltpu.VMEM(first_bias.shape, F32),

time: 104 us -> 73.3 us (0.70)
  the two profiles are of different devices: /device:TPU:15 before, /device:TPU:8 now
where the time goes in v3:
time: 73.3 us; the launch traced here: 72.9 us
  starting transfers between devices  32.5 us (44%)
  Pallas kernels  20.2 us (28%)
  waiting for transfers between devices  19 us (26%)
  local copies, waits for them, and re-layouts  0.94 us (1%)
    all_to_all x1, starting transfers between devices, per_device(): lax.all_to_all(message, 'dom', split_axis=0, concat_axis=0, tiled=True)  17.9 us
    ppermute x3, waiting for transfers between devices, per_device(): lax.ppermute(x, 'scen', [(g, (g + k) % groups) for g in range(groups)])  16.4 us
    ppermute x3, starting transfers between devices, per_device(): lax.ppermute(x, 'scen', [(g, (g + k) % groups) for g in range(groups)])  10.3 us
    pallas_call x1, Pallas kernels, after_halo(): pl.pallas_call(body, out_shape=jax.ShapeDtypeStruct((rows, width), BF16),...  5.71 us
    pallas_call x1, Pallas kernels, ready(): pl.pallas_call(body, out_shape=[pltpu.HBM((tiles, tile, width), BF16), pl...  4.63 us
    all_to_all x1, starting transfers between devices, per_device(): lax.all_to_all(page, 'scen', split_axis=0, concat_axis=0, tiled=True)  4.3 us
    pallas_call x1, Pallas kernels, pick_rows(): pl.pallas_call(body, out_shape=pltpu.HBM((doms, 2 * cap + 8, half), BF16)...  3.83 us
    pallas_call x1, Pallas kernels, pick_tiles(): pl.pallas_call(body, out_shape=[pltpu.HBM((length, width), BF16)] * (grou...  3.03 us
  transfers between devices with their start and end apart: 5, of which 4 were waited for; matrix products, arithmetic and copies ran while one was open for 0% of the time, Pallas kernels for 16%

profile of v3, /device:TPU:8, one launch (start us, length us, event | category | flops | bytes accessed | tf_op | source)
XLA Modules:
  0.0 72.9 jit_solution(4531617843986018197)
XLA Ops:
  0.0 0.0 copy-start
  0.0 0.0 copy-start.7
  0.0 0.0 copy-start.5
  0.0 2.3 %note.1 = bf16[4,16,256]{2,1,0:T(8,128)(2,1)} custom-call(s32[1]{0:T(128)} %bitcast.myself_ref, s32[1,128]{1,0:T(1,128)} %bitcast.18, s32[1,20]{1,0:T(1,128)} %bitcast.14, bf16[2560,256]{1,0:T(8,128)(2,1)} %emb_ref.9), custom_call_target="tpu_custom_call" | custom-call | tf_op jit(solution)/shard_map/note/pallas_call | solution.py:53
  2.3 4.3 %all-to-all-start = ((bf16[4,16,256]{2,1,0:T(8,128)(2,1)}), bf16[4,16,256]{2,1,0:T(8,128)(2,1)S(1)}, u32[]{:S(2)}, u32[]{:S(2)}) async-start(bf16[4,16,256]{2,1,0:T(8,128)(2,1)} %note.1), calls=%async_computation | async-start | bytes 65536 | tf_op jit(solution)/shard_map/all_to_all | solution.py:452
  6.6 0.0 copy-done
  6.6 0.0 copy-done.7
  6.7 0.0 copy-done.5
  6.7 3.8 %pick_rows.1._ = bf16[128,40,128]{2,1,0:T(8,128)(2,1)} custom-call(s32[16,128]{1,0:T(8,128)S(1)} %bitcast.12, s32[1,128]{1,0:T(1,128)S(1)} %bitcast.15, bf16[2560,256]{1,0:T(8,128)(2,1)S(1)} %copy-done), custom_call_target="tpu_custom_call" | custom-call | tf_op jit(solution)/shard_map/pick_rows/pallas_call | solution.py:106
  10.5 1.6 %all-to-all-done.notes_ref = bf16[4,16,256]{2,1,0:T(8,128)(2,1)S(1)} async-done(((bf16[4,16,256]{2,1,0:T(8,128)(2,1)}), bf16[4,16,256]{2,1,0:T(8,128)(2,1)S(1)}, u32[]{:S(2)}, u32[]{:S(2)}) %all-to-all-start) | async-done | bytes 32800 | tf_op jit(solution)/shard_map/all_to_all | solution.py:452
  12.1 0.7 %add_drivers.1 = bf16[128,40,128]{2,1,0:T(8,128)(2,1)} custom-call(bf16[4,16,256]{2,1,0:T(8,128)(2,1)S(1)} %all-to-all-done.notes_ref, bf16[128,40,128]{2,1,0:T(8,128)(2,1)} %pick_rows.1._), custom_call_target="tpu_custom_call", output_to_operand_aliasing={{}: (1, {})} | custom-call | tf_op jit(solution)/shard_map/add_drivers/pallas_call | solution.py:137
  12.8 0.0 copy-start.3
  12.9 0.0 copy-start.4
  12.9 17.9 %all-to-all-start.1 = ((bf16[128,40,128]{2,1,0:T(8,128)(2,1)}), bf16[128,40,128]{2,1,0:T(8,128)(2,1)}, u32[]{:S(2)}, u32[]{:S(2)}) async-start(bf16[128,40,128]{2,1,0:T(8,128)(2,1)} %add_drivers.1), calls=%async_computation.1 | async-start | bytes 2621440 | tf_op jit(solution)/shard_map/all_to_all | solution.py:455
  30.8 0.0 copy-start.11
  30.8 0.0 copy-start.6
  30.8 0.0 copy-done.3
  30.8 0.0 copy-done.4
  30.9 3.0 %pick_tiles.1 = (bf16[832,256]{1,0:T(8,128)(2,1)}, bf16[832,256]{1,0:T(8,128)(2,1)}, bf16[832,256]{1,0:T(8,128)(2,1)}) custom-call(s32[1]{0:T(128)} %bitcast.5.group_ref, s32[4,20]{1,0:T(4,128)S(1)} %bitcast.13, bf16[2560,256]{1,0:T(8,128)(2,1)S(1)} %copy-done, bf16[128,256]{1,0:T(8,128)(2,1)S(1)} %copy-done.3, bf16[64,256]{1,0:T(8,128)(2,1)S(1)} %copy-done.4), custom_call_target="tpu_custom_call" | custom-call | tf_op jit(solution)/shard_map/pick_tiles/pallas_call | solution.py:195
  33.9 2.5 %collective-permute-start = (bf16[832,256]{1,0:T(8,128)(2,1)}, bf16[832,256]{1,0:T(8,128)(2,1)S(1)}, u32[]{:S(2)}, u32[]{:S(2)}) collective-permute-start(bf16[832,256]{1,0:T(8,128)(2,1)} %get-tuple-element.12), channel_id=1, source_target_pairs={{0,1},{1,2},{2,3},{3,0},{4,5},{5,6},{6,7},{7,4},{8,9},{9,10},{10,1... | collective-permute-start | bytes 1277960 | tf_op jit(solution)/shard_map/ppermute | solution.py:460
  36.4 4.5 %collective-permute-start.1 = (bf16[832,256]{1,0:T(8,128)(2,1)}, bf16[832,256]{1,0:T(8,128)(2,1)S(1)}, u32[]{:S(2)}, u32[]{:S(2)}) collective-permute-start(bf16[832,256]{1,0:T(8,128)(2,1)} %get-tuple-element.13), channel_id=1, source_target_pairs={{0,2},{1,3},{2,0},{3,1},{4,6},{5,7},{6,4},{7,5},{8,10},{9,11},{10,... | collective-permute-start | bytes 1277960 | tf_op jit(solution)/shard_map/ppermute | solution.py:460
  40.8 3.4 %collective-permute-start.2 = (bf16[832,256]{1,0:T(8,128)(2,1)}, bf16[832,256]{1,0:T(8,128)(2,1)S(1)}, u32[]{:S(2)}, u32[]{:S(2)}) collective-permute-start(bf16[832,256]{1,0:T(8,128)(2,1)} %get-tuple-element.14), channel_id=1, source_target_pairs={{0,3},{1,0},{2,1},{3,2},{4,7},{5,4},{6,5},{7,6},{8,11},{9,8},{10,9... | collective-permute-start | bytes 1277960 | tf_op jit(solution)/shard_map/ppermute | solution.py:460
  44.2 0.0 copy-done.11
  44.2 0.1 copy.16.at_ref
  44.4 13.8 %collective-permute-done.rest_0_ = bf16[832,256]{1,0:T(8,128)(2,1)S(1)} collective-permute-done((bf16[832,256]{1,0:T(8,128)(2,1)}, bf16[832,256]{1,0:T(8,128)(2,1)S(1)}, u32[]{:S(2)}, u32[]{:S(2)}) %collective-permute-start) | collective-permute-done | bytes 426016 | tf_op jit(solution)/shard_map/ppermute | solution.py:460
  58.2 0.0 copy-start.8
  58.2 0.0 collective-permute-done.1.rest_1_
  58.2 0.0 copy-start.9
  58.2 2.5 %collective-permute-done.2.rest_2_ = bf16[832,256]{1,0:T(8,128)(2,1)S(1)} collective-permute-done((bf16[832,256]{1,0:T(8,128)(2,1)}, bf16[832,256]{1,0:T(8,128)(2,1)S(1)}, u32[]{:S(2)}, u32[]{:S(2)}) %collective-permute-start.2) | collective-permute-done | bytes 426016 | tf_op jit(solution)/shard_map/ppermute | solution.py:460
  60.7 0.0 copy-done.8
  60.7 0.0 copy-done.9
  60.7 0.0 copy-start.10
  60.7 0.8 %copy-done.10 = bf16[832,256]{1,0:T(8,128)(2,1)} copy-done((bf16[832,256]{1,0:T(8,128)(2,1)}, bf16[832,256]{1,0:T(8,128)(2,1)S(1)}, u32[]{:S(2)}) %copy-start.10) | copy-done | bytes 426008
  61.5 0.0 copy-done.6
  61.5 0.0 copy-start.1
  61.5 0.0 copy-start.2
  61.5 4.6 %ready.1 = (bf16[20,128,256]{2,1,0:T(8,128)(2,1)}, f32[2560,256]{1,0:T(8,128)}, bf16[256,256]{1,0:T(8,128)(2,1)}, bf16[256,256]{1,0:T(8,128)(2,1)}) custom-call(s32[1]{0:T(128)} %bitcast.5.group_ref, s32[20]{0:T(128)S(1)} %copy-done.6, bf16[2560,256]{1,0:T(8,128)(2,1)S(1)} %copy-done, bf16[128,256]{1,0:T(8,128)(2,1)} %own_a.1, bf16[64,256]{1,0:T(8,128)(2,1)} %own_b.1, ...), custom_call_target="tpu_custom_call" | custom-call | tf_op jit(solution)/shard_map/ready/pallas_call | solution.py:292
  66.2 1.0 %all-to-all-done.1.halo_hbm = bf16[128,40,128]{2,1,0:T(8,128)(2,1)} async-done(((bf16[128,40,128]{2,1,0:T(8,128)(2,1)}), bf16[128,40,128]{2,1,0:T(8,128)(2,1)}, u32[]{:S(2)}, u32[]{:S(2)}) %all-to-all-start.1) | async-done | bytes 1310752 | tf_op jit(solution)/shard_map/all_to_all | solution.py:455
  67.2 0.0 copy-done.1
  67.2 0.0 copy-done.2
  67.2 5.7 %after_halo.1 = bf16[2560,256]{1,0:T(8,128)(2,1)} custom-call(bf16[128,40,128]{2,1,0:T(8,128)(2,1)} %all-to-all-done.1.halo_hbm, bf16[20,128,256]{2,1,0:T(8,128)(2,1)} %get-tuple-element.15.local_hbm, f32[2560,256]{1,0:T(8,128)} %get-tuple-element.16.start_hbm, bf16[256,256]{1,0:T(8,128)(2,1)} %get-tuple-element.17.lower_hbm, ...), custom_call_target="tpu_custom_call" | custom-call | tf_op jit(solution)/shard_map/after_halo/pallas_call | solution.py:402
  (2 shorter events, 0.0 us)
Async XLA Ops:
  0.0 6.6 %copy-start = (bf16[2560,256]{1,0:T(8,128)(2,1)S(1)}, bf16[2560,256]{1,0:T(8,128)(2,1)}, u32[]{:S(2)}) copy-start(bf16[2560,256]{1,0:T(8,128)(2,1)} %emb_ref.9) | copy-start | bytes 3932164
  0.0 6.6 %copy-start.7 = (s32[128]{0:T(128)S(1)}, s32[128]{0:T(128)}, u32[]{:S(2)}) copy-start(s32[128]{0:T(128)} %param.21) | copy-start | bytes 1540
  0.0 6.6 %copy-start.5 = (s32[128,16]{0,1:T(8,128)S(1)}, s32[128,16]{0,1:T(8,128)}, u32[]{:S(2)}) copy-start(s32[128,16]{0,1:T(8,128)} %param.20) | copy-start | bytes 24580
  2.3 9.8 %all-to-all-start = ((bf16[4,16,256]{2,1,0:T(8,128)(2,1)}), bf16[4,16,256]{2,1,0:T(8,128)(2,1)S(1)}, u32[]{:S(2)}, u32[]{:S(2)}) async-start(bf16[4,16,256]{2,1,0:T(8,128)(2,1)} %note.1), calls=%async_computation | async-start | bytes 65536 | tf_op jit(solution)/shard_map/all_to_all | solution.py:452
  12.8 18.0 %copy-start.3 = (bf16[128,256]{1,0:T(8,128)(2,1)S(1)}, bf16[128,256]{1,0:T(8,128)(2,1)}, u32[]{:S(2)}) copy-start(bf16[128,256]{1,0:T(8,128)(2,1)} %own_a.1) | copy-start | bytes 196612
  12.9 18.0 %copy-start.4 = (bf16[64,256]{1,0:T(8,128)(2,1)S(1)}, bf16[64,256]{1,0:T(8,128)(2,1)}, u32[]{:S(2)}) copy-start(bf16[64,256]{1,0:T(8,128)(2,1)} %own_b.1) | copy-start | bytes 98308
  12.9 54.3 %all-to-all-start.1 = ((bf16[128,40,128]{2,1,0:T(8,128)(2,1)}), bf16[128,40,128]{2,1,0:T(8,128)(2,1)}, u32[]{:S(2)}, u32[]{:S(2)}) async-start(bf16[128,40,128]{2,1,0:T(8,128)(2,1)} %add_drivers.1), calls=%async_computation.1 | async-start | bytes 2621440 | tf_op jit(solution)/shard_map/all_to_all | solution.py:455
  30.8 13.4 %copy-start.11 = (s32[128]{0:T(128)S(1)}, s32[128]{0:T(128)}, u32[]{:S(2)}) copy-start(s32[128]{0:T(128)} %param.22) | copy-start | bytes 1540
  30.8 30.7 %copy-start.6 = (s32[20]{0:T(128)S(1)}, s32[20]{0:T(128)}, u32[]{:S(2)}) copy-start(s32[20]{0:T(128)} %slot_ref.1) | copy-start | bytes 244
  33.9 24.3 %collective-permute-start = (bf16[832,256]{1,0:T(8,128)(2,1)}, bf16[832,256]{1,0:T(8,128)(2,1)S(1)}, u32[]{:S(2)}, u32[]{:S(2)}) collective-permute-start(bf16[832,256]{1,0:T(8,128)(2,1)} %get-tuple-element.12), channel_id=1, source_target_pairs={{0,1},{1,2},{2,3},{3,0},{4,5},{5,6},{6,7},{7,4},{8,9},{9,10},{10,1... | collective-permute-start | bytes 1277960 | tf_op jit(solution)/shard_map/ppermute | solution.py:460
  36.4 21.8 %collective-permute-start.1 = (bf16[832,256]{1,0:T(8,128)(2,1)}, bf16[832,256]{1,0:T(8,128)(2,1)S(1)}, u32[]{:S(2)}, u32[]{:S(2)}) collective-permute-start(bf16[832,256]{1,0:T(8,128)(2,1)} %get-tuple-element.13), channel_id=1, source_target_pairs={{0,2},{1,3},{2,0},{3,1},{4,6},{5,7},{6,4},{7,5},{8,10},{9,11},{10,... | collective-permute-start | bytes 1277960 | tf_op jit(solution)/shard_map/ppermute | solution.py:460
  40.8 19.9 %collective-permute-start.2 = (bf16[832,256]{1,0:T(8,128)(2,1)}, bf16[832,256]{1,0:T(8,128)(2,1)S(1)}, u32[]{:S(2)}, u32[]{:S(2)}) collective-permute-start(bf16[832,256]{1,0:T(8,128)(2,1)} %get-tuple-element.14), channel_id=1, source_target_pairs={{0,3},{1,0},{2,1},{3,2},{4,7},{5,4},{6,5},{7,6},{8,11},{9,8},{10,9... | collective-permute-start | bytes 1277960 | tf_op jit(solution)/shard_map/ppermute | solution.py:460
  58.2 2.5 %copy-start.8 = (bf16[832,256]{1,0:T(8,128)(2,1)}, bf16[832,256]{1,0:T(8,128)(2,1)S(1)}, u32[]{:S(2)}) copy-start(bf16[832,256]{1,0:T(8,128)(2,1)S(1)} %collective-permute-done.rest_0_) | copy-start | bytes 1277956
  58.2 2.5 %copy-start.9 = (bf16[832,256]{1,0:T(8,128)(2,1)}, bf16[832,256]{1,0:T(8,128)(2,1)S(1)}, u32[]{:S(2)}) copy-start(bf16[832,256]{1,0:T(8,128)(2,1)S(1)} %collective-permute-done.1.rest_1_) | copy-start | bytes 1277956
  60.7 0.8 %copy-start.10 = (bf16[832,256]{1,0:T(8,128)(2,1)}, bf16[832,256]{1,0:T(8,128)(2,1)S(1)}, u32[]{:S(2)}) copy-start(bf16[832,256]{1,0:T(8,128)(2,1)S(1)} %collective-permute-done.2.rest_2_) | copy-start | bytes 1277956
  61.5 5.7 %copy-start.1 = (bf16[20,2,128,128]{3,2,1,0:T(8,128)(2,1)S(1)}, bf16[20,2,128,128]{3,2,1,0:T(8,128)(2,1)}, u32[]{:S(2)}) copy-start(bf16[20,2,128,128]{3,2,1,0:T(8,128)(2,1)} %adj_ref.1) | copy-start | bytes 3932164
  61.5 5.7 %copy-start.2 = (bf16[2560,128]{1,0:T(8,128)(2,1)S(1)}, bf16[2560,128]{1,0:T(8,128)(2,1)}, u32[]{:S(2)}) copy-start(bf16[2560,128]{1,0:T(8,128)(2,1)} %dw_ref.1) | copy-start | bytes 1966084

commit v4 on v3

--- a/solution.py
+++ b/solution.py
@@ -169,7 +169,7 @@
 
             def look(t, found, k=k, other=other):
                 tile_at = slots_ref[other, t]
-                hit = tile_at // tiles == me
+                hit = (tile_at >= me * tiles) & (tile_at < (me + 1) * tiles)
 
                 @pl.when(hit)
                 def _():
@@ -206,40 +206,30 @@
     )(group, slots, _near(embedding), first_weight, second_weight)
 
 
-def ready(
-    group, slot, embedding, arrived, first_weight, second_weight, feats, feature_weight, first_bias, tile
-):
-    rows, width = embedding.shape
+def ready(group, slot, embedding, arrived, first_weight, second_weight, tile):
+    width = embedding.shape[1]
     tiles = slot.shape[0]
     groups = len(arrived) + 1
     each = tiles // groups
     a, b = first_weight.shape[0], second_weight.shape[0]
-    many = rows // 4
-
-    def body(group_ref, slot_ref, emb_ref, own_a, own_b, feat_hbm, fw_hbm, bias_hbm, *rest):
+
+    def body(group_ref, slot_ref, emb_ref, own_a, own_b, *rest):
         parts = rest[: groups - 1]
-        tiles_hbm, start_hbm, lower_ref, second_hbm, *rest = rest[groups - 1 :]
-        tiles_ref, start_ref, weight, second_ref, feat_ref, fw_ref, bias_ref, tile_sems, start_sems, sems, small_sems = rest
+        tiles_hbm, first_hbm, second_hbm, tiles_ref, first_ref, second_ref, tile_sems, sems, out_sems = rest[groups - 1 :]
         me = group_ref[0]
-        small = [
-            pltpu.make_async_copy(feat_hbm, feat_ref, small_sems.at[0]),
-            pltpu.make_async_copy(fw_hbm, fw_ref, small_sems.at[1]),
-            pltpu.make_async_copy(bias_hbm, bias_ref, small_sems.at[2]),
-        ]
         firsts, seconds = [], []
         for k in range(groups):
             other = (me + groups - k) % groups
             from_a = own_a if k == 0 else parts[k - 1].at[pl.ds(each * tile, a), :]
             from_b = own_b if k == 0 else parts[k - 1].at[pl.ds(each * tile + a, b), :]
-            to_a = weight.at[pl.ds(pl.multiple_of(other * a, a), a), :]
+            to_a = first_ref.at[pl.ds(pl.multiple_of(other * a, a), a), :]
             to_b = second_ref.at[pl.ds(pl.multiple_of(other * b, b), b), :]
             firsts.append(pltpu.make_async_copy(from_a, to_a, sems.at[0, k]))
             seconds.append(pltpu.make_async_copy(from_b, to_b, sems.at[1, k]))
-        for copy in (*firsts, *small, *seconds):
-            copy.start()
 
         def send(t, counts):
-            source = slot_ref[t] // tiles
+            tile_at = slot_ref[t]
+            source = sum((tile_at >= tiles * g).astype(I32) for g in range(1, groups))
             spot = sum(jnp.where(source == g, counts[g], 0) for g in range(groups))
             away = (me + groups - source) % groups
             for k in range(groups):
@@ -247,43 +237,29 @@
                 @pl.when(away == k)
                 def _(k=k):
                     if k == 0:
-                        at = pl.multiple_of((slot_ref[t] - source * tiles) * tile, tile)
-                        copy = pltpu.make_async_copy(emb_ref.at[pl.ds(at, tile), :], tiles_ref.at[t], tile_sems.at[t])
+                        at = pl.multiple_of((tile_at - source * tiles) * tile, tile)
+                        here = emb_ref.at[pl.ds(at, tile), :]
                     else:
                         at = pl.multiple_of(jnp.minimum(spot, each - 1) * tile, tile)
                         here = parts[k - 1].at[pl.ds(at, tile), :]
-                        copy = pltpu.make_async_copy(here, tiles_ref.at[t], tile_sems.at[t])
-                    copy.start()
+                    pltpu.make_async_copy(here, tiles_ref.at[t], tile_sems.at[t]).start()
 
             return tuple(counts[g] + (source == g).astype(I32) for g in range(groups))
 
         lax.fori_loop(0, tiles, send, (jnp.zeros((), I32),) * groups)
-        for copy in (*firsts, *small):
-            copy.wait()
-        leaving = [pltpu.make_async_copy(weight.at[pl.ds(width, width), :], lower_ref, small_sems.at[0])]
-        leaving[0].start()
-        for n in range(rows // many):
-            here = pl.ds(n * many, many)
-            start_ref[here, :] = (
-                _dot(emb_ref[here, :], weight[:width, :])
-                + lax.dot_general(
-                    feat_ref[:, n * many : (n + 1) * many],
-                    fw_ref[...],
-                    (((0,), (0,)), ((), ())),
-                    preferred_element_type=F32,
-                )
-                + bias_ref[...]
-            )
-            leaving.append(pltpu.make_async_copy(start_ref.at[here, :], start_hbm.at[here, :], start_sems.at[n]))
-            leaving[-1].start()
+        for copy in (*firsts, *seconds):
+            copy.start()
         for t in range(tiles):
             pltpu.make_async_copy(emb_ref.at[pl.ds(0, tile), :], tiles_ref.at[t], tile_sems.at[t]).wait()
-        leaving.append(pltpu.make_async_copy(tiles_ref, tiles_hbm, small_sems.at[1]))
+        leaving = [pltpu.make_async_copy(tiles_ref, tiles_hbm, out_sems.at[0])]
         leaving[-1].start()
-        for copy in seconds:
-            copy.wait()
-        leaving.append(pltpu.make_async_copy(second_ref, second_hbm, small_sems.at[2]))
-        leaving[-1].start()
+        for n, (copies, here, there) in enumerate(
+            ((firsts, first_ref, first_hbm), (seconds, second_ref, second_hbm)), start=1
+        ):
+            for copy in copies:
+                copy.wait()
+            leaving.append(pltpu.make_async_copy(here, there, out_sems.at[n]))
+            leaving[-1].start()
         for copy in leaving:
             copy.wait()
 
@@ -293,86 +269,69 @@
         body,
         out_shape=[
             pltpu.HBM((tiles, tile, width), BF16),
-            pltpu.HBM((rows, width), F32),
-            pltpu.HBM((width, width), BF16),
-            pltpu.HBM((width, width), BF16),
-        ],
-        in_specs=[smem, smem, pl.BlockSpec(memory_space=pltpu.VMEM)] + [hbm] * (5 + len(arrived)),
-        out_specs=[hbm] * 4,
+            pltpu.HBM((groups * a, width), BF16),
+            pltpu.HBM((groups * b, width), BF16),
+        ],
+        in_specs=[smem, smem, pl.BlockSpec(memory_space=pltpu.VMEM)] + [hbm] * (2 + len(arrived)),
+        out_specs=[hbm] * 3,
         scratch_shapes=[
             pltpu.VMEM((tiles, tile, width), BF16),
-            pltpu.VMEM((rows, width), F32),
-            pltpu.VMEM((2 * width, width), BF16),
-            pltpu.VMEM((width, width), BF16),
-            pltpu.VMEM(feats.shape, BF16),
-            pltpu.VMEM(feature_weight.shape, BF16),
-            pltpu.VMEM(first_bias.shape, F32),
+            pltpu.VMEM((groups * a, width), BF16),
+            pltpu.VMEM((groups * b, width), BF16),
             pltpu.SemaphoreType.DMA((tiles,)),
-            pltpu.SemaphoreType.DMA((rows // many,)),
             pltpu.SemaphoreType.DMA((2, groups)),
             pltpu.SemaphoreType.DMA((3,)),
         ],
-        compiler_params=_params(12),
+        compiler_params=_params(4),
         name="ready",
-    )(
-        group,
-        slot,
-        _near(embedding),
-        *map(_far, (first_weight, second_weight, feats, feature_weight, first_bias, *arrived)),
-    )
+    )(group, slot, _near(embedding), *map(_far, (first_weight, second_weight, *arrived)))
 
 
 def after_halo(
-    halo_slot, halo, driver_at, local_tiles, start, adjacency, driver_weight, embedding, lower, second, second_bias
+    halo_slot, halo, driver_at, local_tiles, adjacency, driver_weight, embedding, first, second, feats, feature_weight,
+    first_bias, second_bias,
 ):
     rows, width = embedding.shape
     tiles, _, tile, _ = adjacency.shape
     doms, length, half = halo.shape
     cap = (length - 8) // 2
     hots = driver_weight.shape[1]
-    many = tiles // 4
+    many = tiles // 2
     block = many * tile
     per = tile // cap
 
-    def body(
-        halo_hbm, local_hbm, start_hbm, lower_hbm, second_hbm, slot_hbm, bias_hbm, at_ref, adj_ref, dw_ref, emb_ref,
-        out_hbm, halo_ref, local_ref, start_ref, lower_ref, second_ref, slot_ref, bias_ref, out, sems, in_sems, out_sems,
-    ):
-        halo_copy = pltpu.make_async_copy(halo_hbm, halo_ref, sems.at[0])
-        slot_copy = pltpu.make_async_copy(slot_hbm, slot_ref, sems.at[1])
-        rest = [
-            pltpu.make_async_copy(lower_hbm, lower_ref, sems.at[2]),
-            pltpu.make_async_copy(second_hbm, second_ref, sems.at[3]),
-            pltpu.make_async_copy(bias_hbm, bias_ref, sems.at[4]),
-        ]
+    def body(local_hbm, adj_hbm, *rest):
+        small_hbm, rest = rest[:7], rest[7:]
+        halo_ref, at_ref, dw_ref, emb_ref, out_hbm, local_ref, adj_ref, *rest = rest
+        small, (out, sems, in_sems, out_sems) = rest[:7], rest[7:]
+        slot_ref, first_ref, feat_ref, fw_ref, first_bias_ref, second_ref, second_bias_ref = small
         blocks = tiles // many
-        locals_, starts = [], []
+        smalls = [pltpu.make_async_copy(x, y, sems.at[n]) for n, (x, y) in enumerate(zip(small_hbm, small))]
+        smalls[0].start()
+        arriving = []
         for n in range(blocks):
-            these, here = pl.ds(n * many, many), pl.ds(n * block, block)
-            locals_.append(pltpu.make_async_copy(local_hbm.at[these], local_ref.at[these], in_sems.at[0, n]))
-            starts.append(pltpu.make_async_copy(start_hbm.at[here, :], start_ref.at[here, :], in_sems.at[1, n]))
-        slot_copy.start()
-        halo_copy.start()
-        for n in range(blocks):
-            locals_[n].start()
+            these = pl.ds(n * many, many)
+            arriving.append(
+                (
+                    pltpu.make_async_copy(local_hbm.at[these], local_ref.at[these], in_sems.at[0, n]),
+                    pltpu.make_async_copy(adj_hbm.at[these], adj_ref.at[these], in_sems.at[1, n]),
+                )
+            )
+            for copy in arriving[-1]:
+                copy.start()
             if n == 0:
-                for copy in rest:
+                for copy in smalls[1:]:
                     copy.start()
-            starts[n].start()
-        halo_copy.wait()
         column = lax.broadcasted_iota(I32, (hots, doms * 8), 1)
         ends = halo_ref[:, 2 * cap :, :].reshape(doms * 8, half)
         left = jnp.where(column == at_ref[...], 1.0, 0.0).astype(BF16)
         right = jnp.where(column == at_ref[...] + 4, 1.0, 0.0).astype(BF16)
         drivers = jnp.concatenate([_dot(left, ends).astype(BF16), _dot(right, ends).astype(BF16)], axis=1)
-        slot_copy.wait()
+        smalls[0].wait()
         copies = []
         for n in range(blocks):
-            locals_[n].wait()
-            if n == 0:
-                for copy in rest:
-                    copy.wait()
-            starts[n].wait()
+            for copy in arriving[n]:
+                copy.wait()
             aggregate = []
             for t in range(n * many, (n + 1) * many):
                 which = pl.ds(pl.multiple_of(slot_ref[0, t] * per, per), per)
@@ -386,12 +345,20 @@
                 edges = jnp.concatenate([adj_ref[t, 0], adj_ref[t, 1], dw_ref[t * tile : (t + 1) * tile, :]], axis=1)
                 sources = jnp.concatenate([local_ref[t], halo_tile, drivers], axis=0)
                 aggregate.append(_dot(edges, sources).astype(BF16))
+            if n == 0:
+                for copy in smalls[1:]:
+                    copy.wait()
             here = slice(n * block, (n + 1) * block)
-            inner = start_ref[here, :] + _dot(jnp.concatenate(aggregate, axis=0), lower_ref[...])
+            own = emb_ref[here, :]
+            inner = (
+                _dot(jnp.concatenate([own, jnp.concatenate(aggregate, axis=0)], axis=1), first_ref[...])
+                + lax.dot_general(
+                    feat_ref[:, here], fw_ref[...], (((0,), (0,)), ((), ())), preferred_element_type=F32
+                )
+                + first_bias_ref[...]
+            )
             activated = (0.5 * inner * (1.0 + lax.erf(inner * (0.5**0.5)))).astype(BF16)
-            out[here, :] = (emb_ref[here, :].astype(F32) + bias_ref[...] + _dot(activated, second_ref[...])).astype(
-                BF16
-            )
+            out[here, :] = (own.astype(F32) + second_bias_ref[...] + _dot(activated, second_ref[...])).astype(BF16)
             copies.append(pltpu.make_async_copy(out.at[here, :], out_hbm.at[here, :], out_sems.at[n]))
             copies[-1].start()
         for copy in copies:
@@ -399,29 +366,27 @@
 
     hbm = pl.BlockSpec(memory_space=pltpu.HBM)
     vmem = pl.BlockSpec(memory_space=pltpu.VMEM)
+    smalls = (halo_slot.reshape(1, tiles), first, feats, feature_weight, first_bias, second, second_bias)
     return pl.pallas_call(
         body,
         out_shape=jax.ShapeDtypeStruct((rows, width), BF16),
-        in_specs=[hbm] * 7 + [vmem] * 4,
+        in_specs=[hbm] * 9 + [vmem] * 4,
         out_specs=hbm,
         scratch_shapes=[
-            pltpu.VMEM(halo.shape, BF16),
             pltpu.VMEM(local_tiles.shape, BF16),
-            pltpu.VMEM(start.shape, F32),
-            pltpu.VMEM(lower.shape, BF16),
-            pltpu.VMEM(second.shape, BF16),
+            pltpu.VMEM(adjacency.shape, BF16),
             pltpu.SMEM((1, tiles), I32),
-            pltpu.VMEM(second_bias.shape, F32),
+            *[pltpu.VMEM(x.shape, x.dtype) for x in smalls[1:]],
             pltpu.VMEM((rows, width), BF16),
-            pltpu.SemaphoreType.DMA((5,)),
+            pltpu.SemaphoreType.DMA((7,)),
             pltpu.SemaphoreType.DMA((2, tiles // many)),
             pltpu.SemaphoreType.DMA((tiles // many,)),
         ],
         compiler_params=_params(24),
         name="after_halo",
     )(
-        *map(_far, (halo, local_tiles, start, lower, second, halo_slot.reshape(1, tiles), second_bias)),
-        *map(_near, (driver_at, adjacency, driver_weight, embedding)),
+        *map(_far, (local_tiles, adjacency, *smalls)),
+        *map(_near, (halo, driver_at, driver_weight, embedding)),
     )
 
 
@@ -460,18 +425,7 @@
         lax.ppermute(x, "scen", [(g, (g + k) % groups) for g in range(groups)])
         for k, x in enumerate(leaving, start=1)
     ]
-    local_tiles, start, lower, second = ready(
-        group,
-        local_slot,
-        embedding,
-        arrived,
-        first_weight,
-        second_weight,
-        scenario_feats,
-        feature_weight,
-        first_bias.reshape(1, width),
-        tile,
-    )
+    local_tiles, first, second = ready(group, local_slot, embedding, arrived, first_weight, second_weight, tile)
     owner = hot_ids // rows
     driver_at = (owner // groups * 8 + owner % groups).reshape(-1, 1)
     return after_halo(
@@ -479,12 +433,14 @@
         halo,
         driver_at,
         local_tiles,
-        start,
         adjacency,
         driver_weight,
         embedding,
-        lower,
+        first,
         second,
+        scenario_feats,
+        feature_weight,
+        first_bias.reshape(1, width),
         second_bias.reshape(1, width),
     )
 

time: 73.3 us -> 73 us (level)
  waiting for transfers between devices: 19 us -> 21.6 us
  Pallas kernels: 20.2 us -> 18.4 us
  local copies, waits for them, and re-layouts: 0.94 us -> 0.15 us
    all_to_all x1, waiting for transfers between devices: 1.02 us -> 3.5 us  [per_device(): lax.all_to_all(message, 'dom', split_axis=0, concat_axis=0, tiled=True)]
    pallas_call x1, Pallas kernels: 4.63 us -> 3.67 us  [ready(): pl.pallas_call(body, out_shape=[pltpu.HBM((tiles, tile, width), BF16), pl...]
    unnamed x24 -> x16, local copies, waits for them, and re-layouts: 0.82 us -> 0.04 us
  transfers between devices with their start and end apart: 5 -> 5, of which waited for: 4 -> 4; matrix products, arithmetic and copies ran while one was open for 0% -> 0% of each run, Pallas kernels for 16% -> 14%
where the time goes in v4:
time: 73 us; the launch traced here: 72.5 us
  starting transfers between devices  32.1 us (44%)
  waiting for transfers between devices  21.6 us (30%)
  Pallas kernels  18.4 us (25%)
    all_to_all x1, starting transfers between devices, per_device(): lax.all_to_all(message, 'dom', split_axis=0, concat_axis=0, tiled=True)  17.5 us
    ppermute x3, waiting for transfers between devices, per_device(): lax.ppermute(x, 'scen', [(g, (g + k) % groups) for g in range(groups)])  16.5 us
    ppermute x3, starting transfers between devices, per_device(): lax.ppermute(x, 'scen', [(g, (g + k) % groups) for g in range(groups)])  10.3 us
    pallas_call x1, Pallas kernels, after_halo(): pl.pallas_call(body, out_shape=jax.ShapeDtypeStruct((rows, width), BF16),...  5.43 us
    all_to_all x1, starting transfers between devices, per_device(): lax.all_to_all(page, 'scen', split_axis=0, concat_axis=0, tiled=True)  4.3 us
    pallas_call x1, Pallas kernels, pick_rows(): pl.pallas_call(body, out_shape=pltpu.HBM((doms, 2 * cap + 8, half), BF16)...  3.83 us
    pallas_call x1, Pallas kernels, ready(): pl.pallas_call(body, out_shape=[pltpu.HBM((tiles, tile, width), BF16), pl...  3.67 us
    all_to_all x1, waiting for transfers between devices, per_device(): lax.all_to_all(message, 'dom', split_axis=0, concat_axis=0, tiled=True)  3.5 us
  transfers between devices with their start and end apart: 5, of which 4 were waited for; matrix products, arithmetic and copies ran while one was open for 0% of the time, Pallas kernels for 14%

profile of v4, /device:TPU:8, one launch (start us, length us, event | category | flops | bytes accessed | tf_op | source)
XLA Modules:
  0.0 72.5 jit_solution(15685931066983380424)
XLA Ops:
  0.0 0.0 copy-start
  0.0 0.0 copy-start.4
  0.0 0.0 copy-start.6
  0.0 2.3 %note.1 = bf16[4,16,256]{2,1,0:T(8,128)(2,1)} custom-call(s32[1]{0:T(128)} %bitcast.1.myself_ref, s32[1,128]{1,0:T(1,128)} %bitcast.18, s32[1,20]{1,0:T(1,128)} %bitcast.14, bf16[2560,256]{1,0:T(8,128)(2,1)} %rest_10_.1), custom_call_target="tpu_custom_call" | custom-call | tf_op jit(solution)/shard_map/note/pallas_call | solution.py:53
  2.3 4.3 %all-to-all-start = ((bf16[4,16,256]{2,1,0:T(8,128)(2,1)}), bf16[4,16,256]{2,1,0:T(8,128)(2,1)S(1)}, u32[]{:S(2)}, u32[]{:S(2)}) async-start(bf16[4,16,256]{2,1,0:T(8,128)(2,1)} %note.1), calls=%async_computation | async-start | bytes 65536 | tf_op jit(solution)/shard_map/all_to_all | solution.py:417
  6.6 0.0 copy-done
  6.6 0.0 copy-done.4
  6.6 0.0 copy-done.6
  6.7 3.8 %pick_rows.1._ = bf16[128,40,128]{2,1,0:T(8,128)(2,1)} custom-call(s32[16,128]{1,0:T(8,128)S(1)} %bitcast.12, s32[1,128]{1,0:T(1,128)S(1)} %bitcast.15, bf16[2560,256]{1,0:T(8,128)(2,1)S(1)} %copy-done), custom_call_target="tpu_custom_call" | custom-call | tf_op jit(solution)/shard_map/pick_rows/pallas_call | solution.py:106
  10.5 1.6 %all-to-all-done.notes_ref = bf16[4,16,256]{2,1,0:T(8,128)(2,1)S(1)} async-done(((bf16[4,16,256]{2,1,0:T(8,128)(2,1)}), bf16[4,16,256]{2,1,0:T(8,128)(2,1)S(1)}, u32[]{:S(2)}, u32[]{:S(2)}) %all-to-all-start) | async-done | bytes 32800 | tf_op jit(solution)/shard_map/all_to_all | solution.py:417
  12.1 0.7 %add_drivers.1 = bf16[128,40,128]{2,1,0:T(8,128)(2,1)} custom-call(bf16[4,16,256]{2,1,0:T(8,128)(2,1)S(1)} %all-to-all-done.notes_ref, bf16[128,40,128]{2,1,0:T(8,128)(2,1)} %pick_rows.1._), custom_call_target="tpu_custom_call", output_to_operand_aliasing={{}: (1, {})} | custom-call | tf_op jit(solution)/shard_map/add_drivers/pallas_call | solution.py:137
  12.8 0.0 copy-start.2
  12.8 0.0 copy-start.3
  12.9 17.5 %all-to-all-start.1 = ((bf16[128,40,128]{2,1,0:T(8,128)(2,1)}), bf16[128,40,128]{2,1,0:T(8,128)(2,1)S(1)}, u32[]{:S(2)}, u32[]{:S(2)}) async-start(bf16[128,40,128]{2,1,0:T(8,128)(2,1)} %add_drivers.1), calls=%async_computation.1 | async-start | bytes 2621440 | tf_op jit(solution)/shard_map/all_to_all | solution.py:420
  30.4 0.0 copy-start.7
  30.4 0.0 copy-start.5
  30.4 0.0 copy-done.2
  30.4 0.0 copy-done.3
  30.4 2.5 %pick_tiles.1 = (bf16[832,256]{1,0:T(8,128)(2,1)}, bf16[832,256]{1,0:T(8,128)(2,1)}, bf16[832,256]{1,0:T(8,128)(2,1)}) custom-call(s32[1]{0:T(128)} %bitcast.group_ref, s32[4,20]{1,0:T(4,128)S(1)} %bitcast.13, bf16[2560,256]{1,0:T(8,128)(2,1)S(1)} %copy-done, bf16[128,256]{1,0:T(8,128)(2,1)S(1)} %copy-done.2, bf16[64,256]{1,0:T(8,128)(2,1)S(1)} %copy-done.3), custom_call_target="tpu_custom_call" | custom-call | tf_op jit(solution)/shard_map/pick_tiles/pallas_call | solution.py:195
  32.9 2.5 %collective-permute-start = (bf16[832,256]{1,0:T(8,128)(2,1)}, bf16[832,256]{1,0:T(8,128)(2,1)}, u32[]{:S(2)}, u32[]{:S(2)}) collective-permute-start(bf16[832,256]{1,0:T(8,128)(2,1)} %get-tuple-element.11), channel_id=1, source_target_pairs={{0,1},{1,2},{2,3},{3,0},{4,5},{5,6},{6,7},{7,4},{8,9},{9,10},{10,1... | collective-permute-start | bytes 1277960 | tf_op jit(solution)/shard_map/ppermute | solution.py:425
  35.4 4.5 %collective-permute-start.1 = (bf16[832,256]{1,0:T(8,128)(2,1)}, bf16[832,256]{1,0:T(8,128)(2,1)}, u32[]{:S(2)}, u32[]{:S(2)}) collective-permute-start(bf16[832,256]{1,0:T(8,128)(2,1)} %get-tuple-element.12), channel_id=1, source_target_pairs={{0,2},{1,3},{2,0},{3,1},{4,6},{5,7},{6,4},{7,5},{8,10},{9,11},{10,... | collective-permute-start | bytes 1277960 | tf_op jit(solution)/shard_map/ppermute | solution.py:425
  39.9 3.4 %collective-permute-start.2 = (bf16[832,256]{1,0:T(8,128)(2,1)}, bf16[832,256]{1,0:T(8,128)(2,1)}, u32[]{:S(2)}, u32[]{:S(2)}) collective-permute-start(bf16[832,256]{1,0:T(8,128)(2,1)} %get-tuple-element.13), channel_id=1, source_target_pairs={{0,3},{1,0},{2,1},{3,2},{4,7},{5,4},{6,5},{7,6},{8,11},{9,8},{10,9... | collective-permute-start | bytes 1277960 | tf_op jit(solution)/shard_map/ppermute | solution.py:425
  43.3 0.0 copy-done.7
  43.3 0.1 copy.16.rest_8_
  43.4 0.0 copy-start.1
  43.4 13.9 %collective-permute-done.rest_0_ = bf16[832,256]{1,0:T(8,128)(2,1)} collective-permute-done((bf16[832,256]{1,0:T(8,128)(2,1)}, bf16[832,256]{1,0:T(8,128)(2,1)}, u32[]{:S(2)}, u32[]{:S(2)}) %collective-permute-start) | collective-permute-done | bytes 426016 | tf_op jit(solution)/shard_map/ppermute | solution.py:425
  57.4 0.0 collective-permute-done.1.rest_1_
  57.4 2.5 %collective-permute-done.2.rest_2_ = bf16[832,256]{1,0:T(8,128)(2,1)} collective-permute-done((bf16[832,256]{1,0:T(8,128)(2,1)}, bf16[832,256]{1,0:T(8,128)(2,1)}, u32[]{:S(2)}, u32[]{:S(2)}) %collective-permute-start.2) | collective-permute-done | bytes 426016 | tf_op jit(solution)/shard_map/ppermute | solution.py:425
  59.9 0.0 copy-done.5
  59.9 3.7 %ready.1 = (bf16[20,128,256]{2,1,0:T(8,128)(2,1)}, bf16[512,256]{1,0:T(8,128)(2,1)}, bf16[256,256]{1,0:T(8,128)(2,1)}) custom-call(s32[1]{0:T(128)} %bitcast.group_ref, s32[20]{0:T(128)S(1)} %copy-done.5, bf16[2560,256]{1,0:T(8,128)(2,1)S(1)} %copy-done, bf16[128,256]{1,0:T(8,128)(2,1)} %own_a.1, bf16[64,256]{1,0:T(8,128)(2,1)} %own_b.1, ...), custom_call_target="tpu_custom_call" | custom-call | tf_op jit(solution)/shard_map/ready/pallas_call | solution.py:268
  63.6 3.5 %all-to-all-done.1.rest_7_ = bf16[128,40,128]{2,1,0:T(8,128)(2,1)S(1)} async-done(((bf16[128,40,128]{2,1,0:T(8,128)(2,1)}), bf16[128,40,128]{2,1,0:T(8,128)(2,1)S(1)}, u32[]{:S(2)}, u32[]{:S(2)}) %all-to-all-start.1) | async-done | bytes 1310752 | tf_op jit(solution)/shard_map/all_to_all | solution.py:420
  67.1 0.0 copy-done.1
  67.1 5.4 %after_halo.1 = bf16[2560,256]{1,0:T(8,128)(2,1)} custom-call(bf16[20,128,256]{2,1,0:T(8,128)(2,1)} %get-tuple-element.14.local_hbm, bf16[20,2,128,128]{3,2,1,0:T(8,128)(2,1)} %adj_hbm.1, s32[1,20]{1,0:T(1,128)} %bitcast.19, bf16[512,256]{1,0:T(8,128)(2,1)} %get-tuple-element.15.rest_1_, bf16[16,2560]{1,0:T(8,128)(2,1)} %rest_2_.1, bf16[16,256]{1,0:T(8,128)(2,1)} %rest_3_.1, ...), custom_call_target="tpu_custom_call" | custom-call | tf_op jit(solution)/shard_map/after_halo/pallas_call | solution.py:370
  (2 shorter events, 0.0 us)
Async XLA Ops:
  0.0 6.6 %copy-start = (bf16[2560,256]{1,0:T(8,128)(2,1)S(1)}, bf16[2560,256]{1,0:T(8,128)(2,1)}, u32[]{:S(2)}) copy-start(bf16[2560,256]{1,0:T(8,128)(2,1)} %rest_10_.1) | copy-start | bytes 3932164
  0.0 6.6 %copy-start.4 = (s32[128,16]{0,1:T(8,128)S(1)}, s32[128,16]{0,1:T(8,128)}, u32[]{:S(2)}) copy-start(s32[128,16]{0,1:T(8,128)} %param.20) | copy-start | bytes 24580
  0.0 6.6 %copy-start.6 = (s32[128]{0:T(128)S(1)}, s32[128]{0:T(128)}, u32[]{:S(2)}) copy-start(s32[128]{0:T(128)} %param.21) | copy-start | bytes 1540
  2.3 9.8 %all-to-all-start = ((bf16[4,16,256]{2,1,0:T(8,128)(2,1)}), bf16[4,16,256]{2,1,0:T(8,128)(2,1)S(1)}, u32[]{:S(2)}, u32[]{:S(2)}) async-start(bf16[4,16,256]{2,1,0:T(8,128)(2,1)} %note.1), calls=%async_computation | async-start | bytes 65536 | tf_op jit(solution)/shard_map/all_to_all | solution.py:417
  12.8 17.6 %copy-start.2 = (bf16[128,256]{1,0:T(8,128)(2,1)S(1)}, bf16[128,256]{1,0:T(8,128)(2,1)}, u32[]{:S(2)}) copy-start(bf16[128,256]{1,0:T(8,128)(2,1)} %own_a.1) | copy-start | bytes 196612
  12.8 17.6 %copy-start.3 = (bf16[64,256]{1,0:T(8,128)(2,1)S(1)}, bf16[64,256]{1,0:T(8,128)(2,1)}, u32[]{:S(2)}) copy-start(bf16[64,256]{1,0:T(8,128)(2,1)} %own_b.1) | copy-start | bytes 98308
  12.9 54.2 %all-to-all-start.1 = ((bf16[128,40,128]{2,1,0:T(8,128)(2,1)}), bf16[128,40,128]{2,1,0:T(8,128)(2,1)S(1)}, u32[]{:S(2)}, u32[]{:S(2)}) async-start(bf16[128,40,128]{2,1,0:T(8,128)(2,1)} %add_drivers.1), calls=%async_computation.1 | async-start | bytes 2621440 | tf_op jit(solution)/shard_map/all_to_all | solution.py:420
  30.4 12.9 %copy-start.7 = (s32[128]{0:T(128)S(1)}, s32[128]{0:T(128)}, u32[]{:S(2)}) copy-start(s32[128]{0:T(128)} %param.22) | copy-start | bytes 1540
  30.4 29.5 %copy-start.5 = (s32[20]{0:T(128)S(1)}, s32[20]{0:T(128)}, u32[]{:S(2)}) copy-start(s32[20]{0:T(128)} %slot_ref.1) | copy-start | bytes 244
  32.9 24.4 %collective-permute-start = (bf16[832,256]{1,0:T(8,128)(2,1)}, bf16[832,256]{1,0:T(8,128)(2,1)}, u32[]{:S(2)}, u32[]{:S(2)}) collective-permute-start(bf16[832,256]{1,0:T(8,128)(2,1)} %get-tuple-element.11), channel_id=1, source_target_pairs={{0,1},{1,2},{2,3},{3,0},{4,5},{5,6},{6,7},{7,4},{8,9},{9,10},{10,1... | collective-permute-start | bytes 1277960 | tf_op jit(solution)/shard_map/ppermute | solution.py:425
  35.4 21.9 %collective-permute-start.1 = (bf16[832,256]{1,0:T(8,128)(2,1)}, bf16[832,256]{1,0:T(8,128)(2,1)}, u32[]{:S(2)}, u32[]{:S(2)}) collective-permute-start(bf16[832,256]{1,0:T(8,128)(2,1)} %get-tuple-element.12), channel_id=1, source_target_pairs={{0,2},{1,3},{2,0},{3,1},{4,6},{5,7},{6,4},{7,5},{8,10},{9,11},{10,... | collective-permute-start | bytes 1277960 | tf_op jit(solution)/shard_map/ppermute | solution.py:425
  39.9 20.0 %collective-permute-start.2 = (bf16[832,256]{1,0:T(8,128)(2,1)}, bf16[832,256]{1,0:T(8,128)(2,1)}, u32[]{:S(2)}, u32[]{:S(2)}) collective-permute-start(bf16[832,256]{1,0:T(8,128)(2,1)} %get-tuple-element.13), channel_id=1, source_target_pairs={{0,3},{1,0},{2,1},{3,2},{4,7},{5,4},{6,5},{7,6},{8,11},{9,8},{10,9... | collective-permute-start | bytes 1277960 | tf_op jit(solution)/shard_map/ppermute | solution.py:425
  43.4 23.7 %copy-start.1 = (bf16[2560,128]{1,0:T(8,128)(2,1)S(1)}, bf16[2560,128]{1,0:T(8,128)(2,1)}, u32[]{:S(2)}) copy-start(bf16[2560,128]{1,0:T(8,128)(2,1)} %rest_9_.1) | copy-start | bytes 1966084

commit v5 on v4

--- a/solution.py
+++ b/solution.py
@@ -29,36 +29,36 @@
     rows, width = embedding.shape
     hots, tiles = hot_ids.shape[0], local_slot.shape[0]
 
-    def body(myself_ref, hot_hbm, slot_hbm, emb_ref, out_ref, hot_ref, slot_ref, block, page, sems):
+    def body(myself_ref, hot_hbm, slot_hbm, emb_hbm, out_ref, emb_ref, hot_ref, slot_ref, page, sems):
         hot_copy = pltpu.make_async_copy(hot_hbm, hot_ref, sems.at[0])
         slot_copy = pltpu.make_async_copy(slot_hbm, slot_ref, sems.at[1])
+        emb_copy = pltpu.make_async_copy(emb_hbm, emb_ref, sems.at[2])
         hot_copy.start()
         slot_copy.start()
+        emb_copy.start()
         page[...] = jnp.zeros((NOTE, width), F32)
         hot_copy.wait()
         within = hot_ref[...] - myself_ref[0] * rows
         row = jnp.max(jnp.where((within >= 0) & (within < rows), within, -1))
         start = pl.multiple_of((jnp.maximum(row, 0) // NOTE) * NOTE, NOTE)
-        copy = pltpu.make_async_copy(emb_ref.at[pl.ds(start, NOTE), :], block, sems.at[2])
-        copy.start()
         slot_copy.wait()
         page[1:2, :tiles] = slot_ref[...].astype(F32)
-        copy.wait()
+        emb_copy.wait()
         at = lax.broadcasted_iota(I32, (NOTE, width), 0)
-        mine = jnp.where(at == row - start, block[...].astype(F32), 0.0)
+        mine = jnp.where(at == row - start, emb_ref[pl.ds(start, NOTE), :].astype(F32), 0.0)
         page[0:1, :] = jnp.sum(mine, axis=0, keepdims=True)
         out_ref[...] = jnp.broadcast_to(page[...].astype(BF16)[None], (groups, NOTE, width))
 
     hbm = pl.BlockSpec(memory_space=pltpu.HBM)
-    return pl.pallas_call(
-        body,
-        out_shape=pltpu.VMEM((groups, NOTE, width), BF16),
+    vmem = pl.BlockSpec(memory_space=pltpu.VMEM)
+    return pl.pallas_call(
+        body,
+        out_shape=[pltpu.VMEM((groups, NOTE, width), BF16), pltpu.VMEM((rows, width), BF16)],
         in_specs=[pl.BlockSpec(memory_space=pltpu.SMEM), hbm, hbm, hbm],
-        out_specs=pl.BlockSpec(memory_space=pltpu.VMEM),
+        out_specs=[vmem, vmem],
         scratch_shapes=[
             pltpu.VMEM((1, hots), I32),
             pltpu.VMEM((1, tiles), I32),
-            pltpu.VMEM((NOTE, width), BF16),
             pltpu.VMEM((NOTE, width), F32),
             pltpu.SemaphoreType.DMA((3,)),
         ],
@@ -413,7 +413,7 @@
     myself = lax.axis_index(("dom", "scen")).astype(I32).reshape(1)
     group = lax.axis_index("scen").astype(I32).reshape(1)
 
-    page = note(myself, hot_ids, local_slot, embedding, groups)
+    page, embedding = note(myself, hot_ids, local_slot, embedding, groups)
     notes = lax.all_to_all(page, "scen", split_axis=0, concat_axis=0, tiled=True)
     message = pick_rows(send_rows, send_count, embedding)
     message = add_drivers(notes, message)

time: 73 us -> 72.7 us (level)
  no operation moved by 1% of the time
where the time goes in v5:
time: 72.7 us; the launch traced here: 72.2 us
  starting transfers between devices  32.1 us (44%)
  waiting for transfers between devices  21.3 us (29%)
  Pallas kernels  18.5 us (25%)
    all_to_all x1, starting transfers between devices, per_device(): lax.all_to_all(message, 'dom', split_axis=0, concat_axis=0, tiled=True)  17.5 us
    ppermute x3, waiting for transfers between devices, per_device(): lax.ppermute(x, 'scen', [(g, (g + k) % groups) for g in range(groups)])  16.5 us
    ppermute x3, starting transfers between devices, per_device(): lax.ppermute(x, 'scen', [(g, (g + k) % groups) for g in range(groups)])  10.3 us
    pallas_call x1, Pallas kernels, after_halo(): pl.pallas_call(body, out_shape=jax.ShapeDtypeStruct((rows, width), BF16),...  5.43 us
    all_to_all x1, starting transfers between devices, per_device(): lax.all_to_all(page, 'scen', split_axis=0, concat_axis=0, tiled=True)  4.3 us
    pallas_call x1, Pallas kernels, ready(): pl.pallas_call(body, out_shape=[pltpu.HBM((tiles, tile, width), BF16), pl...  4 us
    pallas_call x1, Pallas kernels, pick_rows(): pl.pallas_call(body, out_shape=pltpu.HBM((doms, 2 * cap + 8, half), BF16)...  3.83 us
    all_to_all x1, waiting for transfers between devices, per_device(): lax.all_to_all(message, 'dom', split_axis=0, concat_axis=0, tiled=True)  3.17 us
  transfers between devices with their start and end apart: 5, of which 4 were waited for; matrix products, arithmetic and copies ran while one was open for 0% of the time, Pallas kernels for 14%

profile of v5, /device:TPU:8, one launch (start us, length us, event | category | flops | bytes accessed | tf_op | source)
XLA Modules:
  0.0 72.2 jit_solution(893217247520624665)
XLA Ops:
  0.0 0.0 copy-start.3
  0.0 0.0 copy-start.5
  0.0 2.0 %note.1 = (bf16[4,16,256]{2,1,0:T(8,128)(2,1)}, bf16[2560,256]{1,0:T(8,128)(2,1)S(1)}) custom-call(s32[1]{0:T(128)} %bitcast.1.myself_ref, s32[1,128]{1,0:T(1,128)} %bitcast.18, s32[1,20]{1,0:T(1,128)} %bitcast.14, bf16[2560,256]{1,0:T(8,128)(2,1)} %emb_hbm.1), custom_call_target="tpu_custom_call" | custom-call | tf_op jit(solution)/shard_map/note/pallas_call | solution.py:54
  2.0 4.3 %all-to-all-start = ((bf16[4,16,256]{2,1,0:T(8,128)(2,1)}), bf16[4,16,256]{2,1,0:T(8,128)(2,1)S(1)}, u32[]{:S(2)}, u32[]{:S(2)}) async-start(bf16[4,16,256]{2,1,0:T(8,128)(2,1)} %get-tuple-element.14), calls=%async_computation | async-start | bytes 65536 | tf_op jit(solution)/shard_map/all_to_all | solution.py:417
  6.3 0.0 copy-done.3
  6.3 0.0 copy-done.5
  6.3 3.8 %pick_rows.1._ = bf16[128,40,128]{2,1,0:T(8,128)(2,1)} custom-call(s32[16,128]{1,0:T(8,128)S(1)} %bitcast.12, s32[1,128]{1,0:T(1,128)S(1)} %bitcast.15, bf16[2560,256]{1,0:T(8,128)(2,1)S(1)} %get-tuple-element.13.emb_ref.rest_10_), custom_call_target="tpu_custom_call" | custom-call | tf_op jit(solution)/shard_map/pick_rows/pallas_call | solution.py:106
  10.2 1.6 %all-to-all-done.notes_ref = bf16[4,16,256]{2,1,0:T(8,128)(2,1)S(1)} async-done(((bf16[4,16,256]{2,1,0:T(8,128)(2,1)}), bf16[4,16,256]{2,1,0:T(8,128)(2,1)S(1)}, u32[]{:S(2)}, u32[]{:S(2)}) %all-to-all-start) | async-done | bytes 32800 | tf_op jit(solution)/shard_map/all_to_all | solution.py:417
  11.8 0.7 %add_drivers.1 = bf16[128,40,128]{2,1,0:T(8,128)(2,1)} custom-call(bf16[4,16,256]{2,1,0:T(8,128)(2,1)S(1)} %all-to-all-done.notes_ref, bf16[128,40,128]{2,1,0:T(8,128)(2,1)} %pick_rows.1._), custom_call_target="tpu_custom_call", output_to_operand_aliasing={{}: (1, {})} | custom-call | tf_op jit(solution)/shard_map/add_drivers/pallas_call | solution.py:137
  12.5 0.0 copy-start.1
  12.6 0.0 copy-start.2
  12.6 17.5 %all-to-all-start.1 = ((bf16[128,40,128]{2,1,0:T(8,128)(2,1)}), bf16[128,40,128]{2,1,0:T(8,128)(2,1)S(1)}, u32[]{:S(2)}, u32[]{:S(2)}) async-start(bf16[128,40,128]{2,1,0:T(8,128)(2,1)} %add_drivers.1), calls=%async_computation.1 | async-start | bytes 2621440 | tf_op jit(solution)/shard_map/all_to_all | solution.py:420
  30.1 0.0 copy-start.6
  30.1 0.0 copy-start.4
  30.1 0.0 copy-done.1
  30.1 0.0 copy-done.2
  30.1 2.5 %pick_tiles.1 = (bf16[832,256]{1,0:T(8,128)(2,1)}, bf16[832,256]{1,0:T(8,128)(2,1)}, bf16[832,256]{1,0:T(8,128)(2,1)}) custom-call(s32[1]{0:T(128)} %bitcast.group_ref, s32[4,20]{1,0:T(4,128)S(1)} %bitcast.13, bf16[2560,256]{1,0:T(8,128)(2,1)S(1)} %get-tuple-element.13.emb_ref.rest_10_, bf16[128,256]{1,0:T(8,128)(2,1)S(1)} %copy-done.1, ...), custom_call_target="tpu_custom_call" | custom-call | tf_op jit(solution)/shard_map/pick_tiles/pallas_call | solution.py:195
  32.6 2.5 %collective-permute-start = (bf16[832,256]{1,0:T(8,128)(2,1)}, bf16[832,256]{1,0:T(8,128)(2,1)}, u32[]{:S(2)}, u32[]{:S(2)}) collective-permute-start(bf16[832,256]{1,0:T(8,128)(2,1)} %get-tuple-element.15), channel_id=1, source_target_pairs={{0,1},{1,2},{2,3},{3,0},{4,5},{5,6},{6,7},{7,4},{8,9},{9,10},{10,1... | collective-permute-start | bytes 1277960 | tf_op jit(solution)/shard_map/ppermute | solution.py:425
  35.1 4.4 %collective-permute-start.1 = (bf16[832,256]{1,0:T(8,128)(2,1)}, bf16[832,256]{1,0:T(8,128)(2,1)}, u32[]{:S(2)}, u32[]{:S(2)}) collective-permute-start(bf16[832,256]{1,0:T(8,128)(2,1)} %get-tuple-element.16), channel_id=1, source_target_pairs={{0,2},{1,3},{2,0},{3,1},{4,6},{5,7},{6,4},{7,5},{8,10},{9,11},{10,... | collective-permute-start | bytes 1277960 | tf_op jit(solution)/shard_map/ppermute | solution.py:425
  39.6 3.4 %collective-permute-start.2 = (bf16[832,256]{1,0:T(8,128)(2,1)}, bf16[832,256]{1,0:T(8,128)(2,1)}, u32[]{:S(2)}, u32[]{:S(2)}) collective-permute-start(bf16[832,256]{1,0:T(8,128)(2,1)} %get-tuple-element.17), channel_id=1, source_target_pairs={{0,3},{1,0},{2,1},{3,2},{4,7},{5,4},{6,5},{7,6},{8,11},{9,8},{10,9... | collective-permute-start | bytes 1277960 | tf_op jit(solution)/shard_map/ppermute | solution.py:425
  43.0 0.0 copy-done.6
  43.0 0.1 copy.16.rest_8_
  43.1 0.0 copy-start
  43.1 13.9 %collective-permute-done.rest_0_ = bf16[832,256]{1,0:T(8,128)(2,1)} collective-permute-done((bf16[832,256]{1,0:T(8,128)(2,1)}, bf16[832,256]{1,0:T(8,128)(2,1)}, u32[]{:S(2)}, u32[]{:S(2)}) %collective-permute-start) | collective-permute-done | bytes 426016 | tf_op jit(solution)/shard_map/ppermute | solution.py:425
  57.1 0.0 collective-permute-done.1.rest_1_
  57.1 2.5 %collective-permute-done.2.rest_2_ = bf16[832,256]{1,0:T(8,128)(2,1)} collective-permute-done((bf16[832,256]{1,0:T(8,128)(2,1)}, bf16[832,256]{1,0:T(8,128)(2,1)}, u32[]{:S(2)}, u32[]{:S(2)}) %collective-permute-start.2) | collective-permute-done | bytes 426016 | tf_op jit(solution)/shard_map/ppermute | solution.py:425
  59.6 0.0 copy-done.4
  59.6 4.0 %ready.1 = (bf16[20,128,256]{2,1,0:T(8,128)(2,1)}, bf16[512,256]{1,0:T(8,128)(2,1)}, bf16[256,256]{1,0:T(8,128)(2,1)}) custom-call(s32[1]{0:T(128)} %bitcast.group_ref, s32[20]{0:T(128)S(1)} %copy-done.4, bf16[2560,256]{1,0:T(8,128)(2,1)S(1)} %get-tuple-element.13.emb_ref.rest_10_, bf16[128,256]{1,0:T(8,128)(2,1)} %own_a.1, bf16[64,256]{1,0:T(8,128)(2,1)} %own_b.1, ...), custom_call_target="tpu_custom_call" | custom-call | tf_op jit(solution)/shard_map/ready/pallas_call | solution.py:268
  63.6 3.2 %all-to-all-done.1.rest_7_ = bf16[128,40,128]{2,1,0:T(8,128)(2,1)S(1)} async-done(((bf16[128,40,128]{2,1,0:T(8,128)(2,1)}), bf16[128,40,128]{2,1,0:T(8,128)(2,1)S(1)}, u32[]{:S(2)}, u32[]{:S(2)}) %all-to-all-start.1) | async-done | bytes 1310752 | tf_op jit(solution)/shard_map/all_to_all | solution.py:420
  66.8 0.0 copy-done
  66.8 5.4 %after_halo.1 = bf16[2560,256]{1,0:T(8,128)(2,1)} custom-call(bf16[20,128,256]{2,1,0:T(8,128)(2,1)} %get-tuple-element.18.local_hbm, bf16[20,2,128,128]{3,2,1,0:T(8,128)(2,1)} %adj_hbm.1, s32[1,20]{1,0:T(1,128)} %bitcast.19, bf16[512,256]{1,0:T(8,128)(2,1)} %get-tuple-element.19.rest_1_, bf16[16,2560]{1,0:T(8,128)(2,1)} %rest_2_.1, bf16[16,256]{1,0:T(8,128)(2,1)} %rest_3_.1, ...), custom_call_target="tpu_custom_call" | custom-call | tf_op jit(solution)/shard_map/after_halo/pallas_call | solution.py:370
  (2 shorter events, 0.0 us)
Async XLA Ops:
  0.0 6.3 %copy-start.3 = (s32[128,16]{0,1:T(8,128)S(1)}, s32[128,16]{0,1:T(8,128)}, u32[]{:S(2)}) copy-start(s32[128,16]{0,1:T(8,128)} %param.20) | copy-start | bytes 24580
  0.0 6.3 %copy-start.5 = (s32[128]{0:T(128)S(1)}, s32[128]{0:T(128)}, u32[]{:S(2)}) copy-start(s32[128]{0:T(128)} %param.21) | copy-start | bytes 1540
  2.0 9.8 %all-to-all-start = ((bf16[4,16,256]{2,1,0:T(8,128)(2,1)}), bf16[4,16,256]{2,1,0:T(8,128)(2,1)S(1)}, u32[]{:S(2)}, u32[]{:S(2)}) async-start(bf16[4,16,256]{2,1,0:T(8,128)(2,1)} %get-tuple-element.14), calls=%async_computation | async-start | bytes 65536 | tf_op jit(solution)/shard_map/all_to_all | solution.py:417
  12.5 17.6 %copy-start.1 = (bf16[128,256]{1,0:T(8,128)(2,1)S(1)}, bf16[128,256]{1,0:T(8,128)(2,1)}, u32[]{:S(2)}) copy-start(bf16[128,256]{1,0:T(8,128)(2,1)} %own_a.1) | copy-start | bytes 196612
  12.6 17.6 %copy-start.2 = (bf16[64,256]{1,0:T(8,128)(2,1)S(1)}, bf16[64,256]{1,0:T(8,128)(2,1)}, u32[]{:S(2)}) copy-start(bf16[64,256]{1,0:T(8,128)(2,1)} %own_b.1) | copy-start | bytes 98308
  12.6 54.2 %all-to-all-start.1 = ((bf16[128,40,128]{2,1,0:T(8,128)(2,1)}), bf16[128,40,128]{2,1,0:T(8,128)(2,1)S(1)}, u32[]{:S(2)}, u32[]{:S(2)}) async-start(bf16[128,40,128]{2,1,0:T(8,128)(2,1)} %add_drivers.1), calls=%async_computation.1 | async-start | bytes 2621440 | tf_op jit(solution)/shard_map/all_to_all | solution.py:420
  30.1 12.9 %copy-start.6 = (s32[128]{0:T(128)S(1)}, s32[128]{0:T(128)}, u32[]{:S(2)}) copy-start(s32[128]{0:T(128)} %param.22) | copy-start | bytes 1540
  30.1 29.5 %copy-start.4 = (s32[20]{0:T(128)S(1)}, s32[20]{0:T(128)}, u32[]{:S(2)}) copy-start(s32[20]{0:T(128)} %slot_ref.1) | copy-start | bytes 244
  32.6 24.4 %collective-permute-start = (bf16[832,256]{1,0:T(8,128)(2,1)}, bf16[832,256]{1,0:T(8,128)(2,1)}, u32[]{:S(2)}, u32[]{:S(2)}) collective-permute-start(bf16[832,256]{1,0:T(8,128)(2,1)} %get-tuple-element.15), channel_id=1, source_target_pairs={{0,1},{1,2},{2,3},{3,0},{4,5},{5,6},{6,7},{7,4},{8,9},{9,10},{10,1... | collective-permute-start | bytes 1277960 | tf_op jit(solution)/shard_map/ppermute | solution.py:425
  35.1 21.9 %collective-permute-start.1 = (bf16[832,256]{1,0:T(8,128)(2,1)}, bf16[832,256]{1,0:T(8,128)(2,1)}, u32[]{:S(2)}, u32[]{:S(2)}) collective-permute-start(bf16[832,256]{1,0:T(8,128)(2,1)} %get-tuple-element.16), channel_id=1, source_target_pairs={{0,2},{1,3},{2,0},{3,1},{4,6},{5,7},{6,4},{7,5},{8,10},{9,11},{10,... | collective-permute-start | bytes 1277960 | tf_op jit(solution)/shard_map/ppermute | solution.py:425
  39.6 20.0 %collective-permute-start.2 = (bf16[832,256]{1,0:T(8,128)(2,1)}, bf16[832,256]{1,0:T(8,128)(2,1)}, u32[]{:S(2)}, u32[]{:S(2)}) collective-permute-start(bf16[832,256]{1,0:T(8,128)(2,1)} %get-tuple-element.17), channel_id=1, source_target_pairs={{0,3},{1,0},{2,1},{3,2},{4,7},{5,4},{6,5},{7,6},{8,11},{9,8},{10,9... | collective-permute-start | bytes 1277960 | tf_op jit(solution)/shard_map/ppermute | solution.py:425
  43.1 23.7 %copy-start = (bf16[2560,128]{1,0:T(8,128)(2,1)S(1)}, bf16[2560,128]{1,0:T(8,128)(2,1)}, u32[]{:S(2)}) copy-start(bf16[2560,128]{1,0:T(8,128)(2,1)} %rest_9_.1) | copy-start | bytes 1966084

commit v6 on v5

--- a/solution.py
+++ b/solution.py
@@ -330,8 +330,9 @@
         smalls[0].wait()
         copies = []
         for n in range(blocks):
-            for copy in arriving[n]:
-                copy.wait()
+            if n == 0:
+                for copy in arriving[0]:
+                    copy.wait()
             aggregate = []
             for t in range(n * many, (n + 1) * many):
                 which = pl.ds(pl.multiple_of(slot_ref[0, t] * per, per), per)
@@ -346,7 +347,7 @@
                 sources = jnp.concatenate([local_ref[t], halo_tile, drivers], axis=0)
                 aggregate.append(_dot(edges, sources).astype(BF16))
             if n == 0:
-                for copy in smalls[1:]:
+                for copy in (*smalls[1:], *arriving[1]):
                     copy.wait()
             here = slice(n * block, (n + 1) * block)
             own = emb_ref[here, :]

time: 72.7 us -> 72.4 us (level)
  no operation moved by 1% of the time
where the time goes in v6:
time: 72.4 us; the launch traced here: 71.8 us
  starting transfers between devices  32.1 us (44%)
  waiting for transfers between devices  21.4 us (30%)
  Pallas kernels  18 us (25%)
    all_to_all x1, starting transfers between devices, per_device(): lax.all_to_all(message, 'dom', split_axis=0, concat_axis=0, tiled=True)  17.5 us
    ppermute x3, waiting for transfers between devices, per_device(): lax.ppermute(x, 'scen', [(g, (g + k) % groups) for g in range(groups)])  16.5 us
    ppermute x3, starting transfers between devices, per_device(): lax.ppermute(x, 'scen', [(g, (g + k) % groups) for g in range(groups)])  10.3 us
    pallas_call x1, Pallas kernels, after_halo(): pl.pallas_call(body, out_shape=jax.ShapeDtypeStruct((rows, width), BF16),...  5.07 us
    all_to_all x1, starting transfers between devices, per_device(): lax.all_to_all(page, 'scen', split_axis=0, concat_axis=0, tiled=True)  4.3 us
    pallas_call x1, Pallas kernels, ready(): pl.pallas_call(body, out_shape=[pltpu.HBM((tiles, tile, width), BF16), pl...  3.88 us
    pallas_call x1, Pallas kernels, pick_rows(): pl.pallas_call(body, out_shape=pltpu.HBM((doms, 2 * cap + 8, half), BF16)...  3.83 us
    all_to_all x1, waiting for transfers between devices, per_device(): lax.all_to_all(message, 'dom', split_axis=0, concat_axis=0, tiled=True)  3.29 us
  transfers between devices with their start and end apart: 5, of which 4 were waited for; matrix products, arithmetic and copies ran while one was open for 0% of the time, Pallas kernels for 14%

profile of v6, /device:TPU:8, one launch (start us, length us, event | category | flops | bytes accessed | tf_op | source)
XLA Modules:
  0.0 71.8 jit_solution(17217103098096290662)
XLA Ops:
  0.0 0.0 copy-start.3
  0.0 0.0 copy-start.5
  0.0 2.0 %note.1 = (bf16[4,16,256]{2,1,0:T(8,128)(2,1)}, bf16[2560,256]{1,0:T(8,128)(2,1)S(1)}) custom-call(s32[1]{0:T(128)} %bitcast.1.myself_ref, s32[1,128]{1,0:T(1,128)} %bitcast.18, s32[1,20]{1,0:T(1,128)} %bitcast.14, bf16[2560,256]{1,0:T(8,128)(2,1)} %emb_hbm.1), custom_call_target="tpu_custom_call" | custom-call | tf_op jit(solution)/shard_map/note/pallas_call | solution.py:54
  2.0 4.3 %all-to-all-start = ((bf16[4,16,256]{2,1,0:T(8,128)(2,1)}), bf16[4,16,256]{2,1,0:T(8,128)(2,1)S(1)}, u32[]{:S(2)}, u32[]{:S(2)}) async-start(bf16[4,16,256]{2,1,0:T(8,128)(2,1)} %get-tuple-element.14), calls=%async_computation | async-start | bytes 65536 | tf_op jit(solution)/shard_map/all_to_all | solution.py:418
  6.3 0.0 copy-done.3
  6.3 0.0 copy-done.5
  6.3 3.8 %pick_rows.1._ = bf16[128,40,128]{2,1,0:T(8,128)(2,1)} custom-call(s32[16,128]{1,0:T(8,128)S(1)} %bitcast.12, s32[1,128]{1,0:T(1,128)S(1)} %bitcast.15, bf16[2560,256]{1,0:T(8,128)(2,1)S(1)} %get-tuple-element.13.emb_ref.rest_10_), custom_call_target="tpu_custom_call" | custom-call | tf_op jit(solution)/shard_map/pick_rows/pallas_call | solution.py:106
  10.2 1.6 %all-to-all-done.notes_ref = bf16[4,16,256]{2,1,0:T(8,128)(2,1)S(1)} async-done(((bf16[4,16,256]{2,1,0:T(8,128)(2,1)}), bf16[4,16,256]{2,1,0:T(8,128)(2,1)S(1)}, u32[]{:S(2)}, u32[]{:S(2)}) %all-to-all-start) | async-done | bytes 32800 | tf_op jit(solution)/shard_map/all_to_all | solution.py:418
  11.8 0.7 %add_drivers.1 = bf16[128,40,128]{2,1,0:T(8,128)(2,1)} custom-call(bf16[4,16,256]{2,1,0:T(8,128)(2,1)S(1)} %all-to-all-done.notes_ref, bf16[128,40,128]{2,1,0:T(8,128)(2,1)} %pick_rows.1._), custom_call_target="tpu_custom_call", output_to_operand_aliasing={{}: (1, {})} | custom-call | tf_op jit(solution)/shard_map/add_drivers/pallas_call | solution.py:137
  12.5 0.0 copy-start.1
  12.6 0.0 copy-start.2
  12.6 17.5 %all-to-all-start.1 = ((bf16[128,40,128]{2,1,0:T(8,128)(2,1)}), bf16[128,40,128]{2,1,0:T(8,128)(2,1)S(1)}, u32[]{:S(2)}, u32[]{:S(2)}) async-start(bf16[128,40,128]{2,1,0:T(8,128)(2,1)} %add_drivers.1), calls=%async_computation.1 | async-start | bytes 2621440 | tf_op jit(solution)/shard_map/all_to_all | solution.py:421
  30.1 0.0 copy-start.6
  30.1 0.0 copy-start.4
  30.1 0.0 copy-done.1
  30.1 0.0 copy-done.2
  30.1 2.5 %pick_tiles.1 = (bf16[832,256]{1,0:T(8,128)(2,1)}, bf16[832,256]{1,0:T(8,128)(2,1)}, bf16[832,256]{1,0:T(8,128)(2,1)}) custom-call(s32[1]{0:T(128)} %bitcast.group_ref, s32[4,20]{1,0:T(4,128)S(1)} %bitcast.13, bf16[2560,256]{1,0:T(8,128)(2,1)S(1)} %get-tuple-element.13.emb_ref.rest_10_, bf16[128,256]{1,0:T(8,128)(2,1)S(1)} %copy-done.1, ...), custom_call_target="tpu_custom_call" | custom-call | tf_op jit(solution)/shard_map/pick_tiles/pallas_call | solution.py:195
  32.6 2.5 %collective-permute-start = (bf16[832,256]{1,0:T(8,128)(2,1)}, bf16[832,256]{1,0:T(8,128)(2,1)}, u32[]{:S(2)}, u32[]{:S(2)}) collective-permute-start(bf16[832,256]{1,0:T(8,128)(2,1)} %get-tuple-element.15), channel_id=1, source_target_pairs={{0,1},{1,2},{2,3},{3,0},{4,5},{5,6},{6,7},{7,4},{8,9},{9,10},{10,1... | collective-permute-start | bytes 1277960 | tf_op jit(solution)/shard_map/ppermute | solution.py:426
  35.1 4.4 %collective-permute-start.1 = (bf16[832,256]{1,0:T(8,128)(2,1)}, bf16[832,256]{1,0:T(8,128)(2,1)}, u32[]{:S(2)}, u32[]{:S(2)}) collective-permute-start(bf16[832,256]{1,0:T(8,128)(2,1)} %get-tuple-element.16), channel_id=1, source_target_pairs={{0,2},{1,3},{2,0},{3,1},{4,6},{5,7},{6,4},{7,5},{8,10},{9,11},{10,... | collective-permute-start | bytes 1277960 | tf_op jit(solution)/shard_map/ppermute | solution.py:426
  39.6 3.4 %collective-permute-start.2 = (bf16[832,256]{1,0:T(8,128)(2,1)}, bf16[832,256]{1,0:T(8,128)(2,1)}, u32[]{:S(2)}, u32[]{:S(2)}) collective-permute-start(bf16[832,256]{1,0:T(8,128)(2,1)} %get-tuple-element.17), channel_id=1, source_target_pairs={{0,3},{1,0},{2,1},{3,2},{4,7},{5,4},{6,5},{7,6},{8,11},{9,8},{10,9... | collective-permute-start | bytes 1277960 | tf_op jit(solution)/shard_map/ppermute | solution.py:426
  43.0 0.0 copy-done.6
  43.0 0.1 copy.16.rest_8_
  43.1 0.0 copy-start
  43.1 13.9 %collective-permute-done.rest_0_ = bf16[832,256]{1,0:T(8,128)(2,1)} collective-permute-done((bf16[832,256]{1,0:T(8,128)(2,1)}, bf16[832,256]{1,0:T(8,128)(2,1)}, u32[]{:S(2)}, u32[]{:S(2)}) %collective-permute-start) | collective-permute-done | bytes 426016 | tf_op jit(solution)/shard_map/ppermute | solution.py:426
  57.1 0.0 collective-permute-done.1.rest_1_
  57.1 2.5 %collective-permute-done.2.rest_2_ = bf16[832,256]{1,0:T(8,128)(2,1)} collective-permute-done((bf16[832,256]{1,0:T(8,128)(2,1)}, bf16[832,256]{1,0:T(8,128)(2,1)}, u32[]{:S(2)}, u32[]{:S(2)}) %collective-permute-start.2) | collective-permute-done | bytes 426016 | tf_op jit(solution)/shard_map/ppermute | solution.py:426
  59.6 0.0 copy-done.4
  59.6 3.9 %ready.1 = (bf16[20,128,256]{2,1,0:T(8,128)(2,1)}, bf16[512,256]{1,0:T(8,128)(2,1)}, bf16[256,256]{1,0:T(8,128)(2,1)}) custom-call(s32[1]{0:T(128)} %bitcast.group_ref, s32[20]{0:T(128)S(1)} %copy-done.4, bf16[2560,256]{1,0:T(8,128)(2,1)S(1)} %get-tuple-element.13.emb_ref.rest_10_, bf16[128,256]{1,0:T(8,128)(2,1)} %own_a.1, bf16[64,256]{1,0:T(8,128)(2,1)} %own_b.1, ...), custom_call_target="tpu_custom_call" | custom-call | tf_op jit(solution)/shard_map/ready/pallas_call | solution.py:268
  63.5 3.3 %all-to-all-done.1.rest_7_ = bf16[128,40,128]{2,1,0:T(8,128)(2,1)S(1)} async-done(((bf16[128,40,128]{2,1,0:T(8,128)(2,1)}), bf16[128,40,128]{2,1,0:T(8,128)(2,1)S(1)}, u32[]{:S(2)}, u32[]{:S(2)}) %all-to-all-start.1) | async-done | bytes 1310752 | tf_op jit(solution)/shard_map/all_to_all | solution.py:421
  66.8 0.0 copy-done
  66.8 5.1 %after_halo.1 = bf16[2560,256]{1,0:T(8,128)(2,1)} custom-call(bf16[20,128,256]{2,1,0:T(8,128)(2,1)} %get-tuple-element.18.local_hbm, bf16[20,2,128,128]{3,2,1,0:T(8,128)(2,1)} %adj_hbm.1, s32[1,20]{1,0:T(1,128)} %bitcast.19, bf16[512,256]{1,0:T(8,128)(2,1)} %get-tuple-element.19.rest_1_, bf16[16,2560]{1,0:T(8,128)(2,1)} %rest_2_.1, bf16[16,256]{1,0:T(8,128)(2,1)} %rest_3_.1, ...), custom_call_target="tpu_custom_call" | custom-call | tf_op jit(solution)/shard_map/after_halo/pallas_call | solution.py:371
  (2 shorter events, 0.0 us)
Async XLA Ops:
  0.0 6.3 %copy-start.3 = (s32[128,16]{0,1:T(8,128)S(1)}, s32[128,16]{0,1:T(8,128)}, u32[]{:S(2)}) copy-start(s32[128,16]{0,1:T(8,128)} %param.20) | copy-start | bytes 24580
  0.0 6.3 %copy-start.5 = (s32[128]{0:T(128)S(1)}, s32[128]{0:T(128)}, u32[]{:S(2)}) copy-start(s32[128]{0:T(128)} %param.21) | copy-start | bytes 1540
  2.0 9.8 %all-to-all-start = ((bf16[4,16,256]{2,1,0:T(8,128)(2,1)}), bf16[4,16,256]{2,1,0:T(8,128)(2,1)S(1)}, u32[]{:S(2)}, u32[]{:S(2)}) async-start(bf16[4,16,256]{2,1,0:T(8,128)(2,1)} %get-tuple-element.14), calls=%async_computation | async-start | bytes 65536 | tf_op jit(solution)/shard_map/all_to_all | solution.py:418
  12.5 17.6 %copy-start.1 = (bf16[128,256]{1,0:T(8,128)(2,1)S(1)}, bf16[128,256]{1,0:T(8,128)(2,1)}, u32[]{:S(2)}) copy-start(bf16[128,256]{1,0:T(8,128)(2,1)} %own_a.1) | copy-start | bytes 196612
  12.6 17.6 %copy-start.2 = (bf16[64,256]{1,0:T(8,128)(2,1)S(1)}, bf16[64,256]{1,0:T(8,128)(2,1)}, u32[]{:S(2)}) copy-start(bf16[64,256]{1,0:T(8,128)(2,1)} %own_b.1) | copy-start | bytes 98308
  12.6 54.2 %all-to-all-start.1 = ((bf16[128,40,128]{2,1,0:T(8,128)(2,1)}), bf16[128,40,128]{2,1,0:T(8,128)(2,1)S(1)}, u32[]{:S(2)}, u32[]{:S(2)}) async-start(bf16[128,40,128]{2,1,0:T(8,128)(2,1)} %add_drivers.1), calls=%async_computation.1 | async-start | bytes 2621440 | tf_op jit(solution)/shard_map/all_to_all | solution.py:421
  30.1 12.9 %copy-start.6 = (s32[128]{0:T(128)S(1)}, s32[128]{0:T(128)}, u32[]{:S(2)}) copy-start(s32[128]{0:T(128)} %param.22) | copy-start | bytes 1540
  30.1 29.5 %copy-start.4 = (s32[20]{0:T(128)S(1)}, s32[20]{0:T(128)}, u32[]{:S(2)}) copy-start(s32[20]{0:T(128)} %slot_ref.1) | copy-start | bytes 244
  32.6 24.4 %collective-permute-start = (bf16[832,256]{1,0:T(8,128)(2,1)}, bf16[832,256]{1,0:T(8,128)(2,1)}, u32[]{:S(2)}, u32[]{:S(2)}) collective-permute-start(bf16[832,256]{1,0:T(8,128)(2,1)} %get-tuple-element.15), channel_id=1, source_target_pairs={{0,1},{1,2},{2,3},{3,0},{4,5},{5,6},{6,7},{7,4},{8,9},{9,10},{10,1... | collective-permute-start | bytes 1277960 | tf_op jit(solution)/shard_map/ppermute | solution.py:426
  35.1 21.9 %collective-permute-start.1 = (bf16[832,256]{1,0:T(8,128)(2,1)}, bf16[832,256]{1,0:T(8,128)(2,1)}, u32[]{:S(2)}, u32[]{:S(2)}) collective-permute-start(bf16[832,256]{1,0:T(8,128)(2,1)} %get-tuple-element.16), channel_id=1, source_target_pairs={{0,2},{1,3},{2,0},{3,1},{4,6},{5,7},{6,4},{7,5},{8,10},{9,11},{10,... | collective-permute-start | bytes 1277960 | tf_op jit(solution)/shard_map/ppermute | solution.py:426
  39.6 20.0 %collective-permute-start.2 = (bf16[832,256]{1,0:T(8,128)(2,1)}, bf16[832,256]{1,0:T(8,128)(2,1)}, u32[]{:S(2)}, u32[]{:S(2)}) collective-permute-start(bf16[832,256]{1,0:T(8,128)(2,1)} %get-tuple-element.17), channel_id=1, source_target_pairs={{0,3},{1,0},{2,1},{3,2},{4,7},{5,4},{6,5},{7,6},{8,11},{9,8},{10,9... | collective-permute-start | bytes 1277960 | tf_op jit(solution)/shard_map/ppermute | solution.py:426
  43.1 23.7 %copy-start = (bf16[2560,128]{1,0:T(8,128)(2,1)S(1)}, bf16[2560,128]{1,0:T(8,128)(2,1)}, u32[]{:S(2)}) copy-start(bf16[2560,128]{1,0:T(8,128)(2,1)} %rest_9_.1) | copy-start | bytes 1966084

commit v7 on v6

--- a/solution.py
+++ b/solution.py
@@ -359,9 +359,16 @@
                 + first_bias_ref[...]
             )
             activated = (0.5 * inner * (1.0 + lax.erf(inner * (0.5**0.5)))).astype(BF16)
-            out[here, :] = (own.astype(F32) + second_bias_ref[...] + _dot(activated, second_ref[...])).astype(BF16)
-            copies.append(pltpu.make_async_copy(out.at[here, :], out_hbm.at[here, :], out_sems.at[n]))
-            copies[-1].start()
+            part = block // 2
+            for h in range(2):
+                there = slice(n * block + h * part, n * block + (h + 1) * part)
+                out[there, :] = (
+                    own[h * part : (h + 1) * part].astype(F32)
+                    + second_bias_ref[...]
+                    + _dot(activated[h * part : (h + 1) * part], second_ref[...])
+                ).astype(BF16)
+                copies.append(pltpu.make_async_copy(out.at[there, :], out_hbm.at[there, :], out_sems.at[2 * n + h]))
+                copies[-1].start()
         for copy in copies:
             copy.wait()
 
@@ -381,7 +388,7 @@
             pltpu.VMEM((rows, width), BF16),
             pltpu.SemaphoreType.DMA((7,)),
             pltpu.SemaphoreType.DMA((2, tiles // many)),
-            pltpu.SemaphoreType.DMA((tiles // many,)),
+            pltpu.SemaphoreType.DMA((2 * (tiles // many),)),
         ],
         compiler_params=_params(24),
         name="after_halo",

time: 72.4 us -> 72.3 us (level)
  no operation moved by 1% of the time
where the time goes in v7:
time: 72.3 us; the launch traced here: 71.8 us
  starting transfers between devices  32.1 us (44%)
  waiting for transfers between devices  21.3 us (29%)
  Pallas kernels  18.1 us (25%)
    all_to_all x1, starting transfers between devices, per_device(): lax.all_to_all(message, 'dom', split_axis=0, concat_axis=0, tiled=True)  17.5 us
    ppermute x3, waiting for transfers between devices, per_device(): lax.ppermute(x, 'scen', [(g, (g + k) % groups) for g in range(groups)])  16.5 us
    ppermute x3, starting transfers between devices, per_device(): lax.ppermute(x, 'scen', [(g, (g + k) % groups) for g in range(groups)])  10.3 us
    pallas_call x1, Pallas kernels, after_halo(): pl.pallas_call(body, out_shape=jax.ShapeDtypeStruct((rows, width), BF16),...  4.98 us
    all_to_all x1, starting transfers between devices, per_device(): lax.all_to_all(page, 'scen', split_axis=0, concat_axis=0, tiled=True)  4.3 us
    pallas_call x1, Pallas kernels, ready(): pl.pallas_call(body, out_shape=[pltpu.HBM((tiles, tile, width), BF16), pl...  4.01 us
    pallas_call x1, Pallas kernels, pick_rows(): pl.pallas_call(body, out_shape=pltpu.HBM((doms, 2 * cap + 8, half), BF16)...  3.83 us
    all_to_all x1, waiting for transfers between devices, per_device(): lax.all_to_all(message, 'dom', split_axis=0, concat_axis=0, tiled=True)  3.16 us
  transfers between devices with their start and end apart: 5, of which 4 were waited for; matrix products, arithmetic and copies ran while one was open for 0% of the time, Pallas kernels for 14%

profile of v7, /device:TPU:8, one launch (start us, length us, event | category | flops | bytes accessed | tf_op | source)
XLA Modules:
  0.0 71.8 jit_solution(18290244118494072138)
XLA Ops:
  0.0 0.0 copy-start.3
  0.0 0.0 copy-start.5
  0.0 2.0 %note.1 = (bf16[4,16,256]{2,1,0:T(8,128)(2,1)}, bf16[2560,256]{1,0:T(8,128)(2,1)S(1)}) custom-call(s32[1]{0:T(128)} %bitcast.1.myself_ref, s32[1,128]{1,0:T(1,128)} %bitcast.18, s32[1,20]{1,0:T(1,128)} %bitcast.14, bf16[2560,256]{1,0:T(8,128)(2,1)} %emb_hbm.1), custom_call_target="tpu_custom_call" | custom-call | tf_op jit(solution)/shard_map/note/pallas_call | solution.py:54
  2.0 4.3 %all-to-all-start = ((bf16[4,16,256]{2,1,0:T(8,128)(2,1)}), bf16[4,16,256]{2,1,0:T(8,128)(2,1)S(1)}, u32[]{:S(2)}, u32[]{:S(2)}) async-start(bf16[4,16,256]{2,1,0:T(8,128)(2,1)} %get-tuple-element.14), calls=%async_computation | async-start | bytes 65536 | tf_op jit(solution)/shard_map/all_to_all | solution.py:425
  6.3 0.0 copy-done.3
  6.3 0.0 copy-done.5
  6.3 3.8 %pick_rows.1._ = bf16[128,40,128]{2,1,0:T(8,128)(2,1)} custom-call(s32[16,128]{1,0:T(8,128)S(1)} %bitcast.12, s32[1,128]{1,0:T(1,128)S(1)} %bitcast.15, bf16[2560,256]{1,0:T(8,128)(2,1)S(1)} %get-tuple-element.13.emb_ref.rest_10_), custom_call_target="tpu_custom_call" | custom-call | tf_op jit(solution)/shard_map/pick_rows/pallas_call | solution.py:106
  10.2 1.6 %all-to-all-done.notes_ref = bf16[4,16,256]{2,1,0:T(8,128)(2,1)S(1)} async-done(((bf16[4,16,256]{2,1,0:T(8,128)(2,1)}), bf16[4,16,256]{2,1,0:T(8,128)(2,1)S(1)}, u32[]{:S(2)}, u32[]{:S(2)}) %all-to-all-start) | async-done | bytes 32800 | tf_op jit(solution)/shard_map/all_to_all | solution.py:425
  11.8 0.7 %add_drivers.1 = bf16[128,40,128]{2,1,0:T(8,128)(2,1)} custom-call(bf16[4,16,256]{2,1,0:T(8,128)(2,1)S(1)} %all-to-all-done.notes_ref, bf16[128,40,128]{2,1,0:T(8,128)(2,1)} %pick_rows.1._), custom_call_target="tpu_custom_call", output_to_operand_aliasing={{}: (1, {})} | custom-call | tf_op jit(solution)/shard_map/add_drivers/pallas_call | solution.py:137
  12.5 0.0 copy-start.1
  12.6 0.0 copy-start.2
  12.6 17.5 %all-to-all-start.1 = ((bf16[128,40,128]{2,1,0:T(8,128)(2,1)}), bf16[128,40,128]{2,1,0:T(8,128)(2,1)S(1)}, u32[]{:S(2)}, u32[]{:S(2)}) async-start(bf16[128,40,128]{2,1,0:T(8,128)(2,1)} %add_drivers.1), calls=%async_computation.1 | async-start | bytes 2621440 | tf_op jit(solution)/shard_map/all_to_all | solution.py:428
  30.1 0.0 copy-start.6
  30.1 0.0 copy-start.4
  30.1 0.0 copy-done.1
  30.1 0.0 copy-done.2
  30.1 2.5 %pick_tiles.1 = (bf16[832,256]{1,0:T(8,128)(2,1)}, bf16[832,256]{1,0:T(8,128)(2,1)}, bf16[832,256]{1,0:T(8,128)(2,1)}) custom-call(s32[1]{0:T(128)} %bitcast.group_ref, s32[4,20]{1,0:T(4,128)S(1)} %bitcast.13, bf16[2560,256]{1,0:T(8,128)(2,1)S(1)} %get-tuple-element.13.emb_ref.rest_10_, bf16[128,256]{1,0:T(8,128)(2,1)S(1)} %copy-done.1, ...), custom_call_target="tpu_custom_call" | custom-call | tf_op jit(solution)/shard_map/pick_tiles/pallas_call | solution.py:195
  32.6 2.5 %collective-permute-start = (bf16[832,256]{1,0:T(8,128)(2,1)}, bf16[832,256]{1,0:T(8,128)(2,1)}, u32[]{:S(2)}, u32[]{:S(2)}) collective-permute-start(bf16[832,256]{1,0:T(8,128)(2,1)} %get-tuple-element.15), channel_id=1, source_target_pairs={{0,1},{1,2},{2,3},{3,0},{4,5},{5,6},{6,7},{7,4},{8,9},{9,10},{10,1... | collective-permute-start | bytes 1277960 | tf_op jit(solution)/shard_map/ppermute | solution.py:433
  35.1 4.4 %collective-permute-start.1 = (bf16[832,256]{1,0:T(8,128)(2,1)}, bf16[832,256]{1,0:T(8,128)(2,1)}, u32[]{:S(2)}, u32[]{:S(2)}) collective-permute-start(bf16[832,256]{1,0:T(8,128)(2,1)} %get-tuple-element.16), channel_id=1, source_target_pairs={{0,2},{1,3},{2,0},{3,1},{4,6},{5,7},{6,4},{7,5},{8,10},{9,11},{10,... | collective-permute-start | bytes 1277960 | tf_op jit(solution)/shard_map/ppermute | solution.py:433
  39.6 3.4 %collective-permute-start.2 = (bf16[832,256]{1,0:T(8,128)(2,1)}, bf16[832,256]{1,0:T(8,128)(2,1)}, u32[]{:S(2)}, u32[]{:S(2)}) collective-permute-start(bf16[832,256]{1,0:T(8,128)(2,1)} %get-tuple-element.17), channel_id=1, source_target_pairs={{0,3},{1,0},{2,1},{3,2},{4,7},{5,4},{6,5},{7,6},{8,11},{9,8},{10,9... | collective-permute-start | bytes 1277960 | tf_op jit(solution)/shard_map/ppermute | solution.py:433
  43.0 0.0 copy-done.6
  43.0 0.1 copy.16.rest_8_
  43.1 0.0 copy-start
  43.1 13.9 %collective-permute-done.rest_0_ = bf16[832,256]{1,0:T(8,128)(2,1)} collective-permute-done((bf16[832,256]{1,0:T(8,128)(2,1)}, bf16[832,256]{1,0:T(8,128)(2,1)}, u32[]{:S(2)}, u32[]{:S(2)}) %collective-permute-start) | collective-permute-done | bytes 426016 | tf_op jit(solution)/shard_map/ppermute | solution.py:433
  57.1 0.0 collective-permute-done.1.rest_1_
  57.1 2.5 %collective-permute-done.2.rest_2_ = bf16[832,256]{1,0:T(8,128)(2,1)} collective-permute-done((bf16[832,256]{1,0:T(8,128)(2,1)}, bf16[832,256]{1,0:T(8,128)(2,1)}, u32[]{:S(2)}, u32[]{:S(2)}) %collective-permute-start.2) | collective-permute-done | bytes 426016 | tf_op jit(solution)/shard_map/ppermute | solution.py:433
  59.6 0.0 copy-done.4
  59.6 4.0 %ready.1 = (bf16[20,128,256]{2,1,0:T(8,128)(2,1)}, bf16[512,256]{1,0:T(8,128)(2,1)}, bf16[256,256]{1,0:T(8,128)(2,1)}) custom-call(s32[1]{0:T(128)} %bitcast.group_ref, s32[20]{0:T(128)S(1)} %copy-done.4, bf16[2560,256]{1,0:T(8,128)(2,1)S(1)} %get-tuple-element.13.emb_ref.rest_10_, bf16[128,256]{1,0:T(8,128)(2,1)} %own_a.1, bf16[64,256]{1,0:T(8,128)(2,1)} %own_b.1, ...), custom_call_target="tpu_custom_call" | custom-call | tf_op jit(solution)/shard_map/ready/pallas_call | solution.py:268
  63.6 3.2 %all-to-all-done.1.rest_7_ = bf16[128,40,128]{2,1,0:T(8,128)(2,1)S(1)} async-done(((bf16[128,40,128]{2,1,0:T(8,128)(2,1)}), bf16[128,40,128]{2,1,0:T(8,128)(2,1)S(1)}, u32[]{:S(2)}, u32[]{:S(2)}) %all-to-all-start.1) | async-done | bytes 1310752 | tf_op jit(solution)/shard_map/all_to_all | solution.py:428
  66.8 0.0 copy-done
  66.8 5.0 %after_halo.1 = bf16[2560,256]{1,0:T(8,128)(2,1)} custom-call(bf16[20,128,256]{2,1,0:T(8,128)(2,1)} %get-tuple-element.18.local_hbm, bf16[20,2,128,128]{3,2,1,0:T(8,128)(2,1)} %adj_hbm.1, s32[1,20]{1,0:T(1,128)} %bitcast.19, bf16[512,256]{1,0:T(8,128)(2,1)} %get-tuple-element.19.rest_1_, bf16[16,2560]{1,0:T(8,128)(2,1)} %rest_2_.1, bf16[16,256]{1,0:T(8,128)(2,1)} %rest_3_.1, ...), custom_call_target="tpu_custom_call" | custom-call | tf_op jit(solution)/shard_map/after_halo/pallas_call | solution.py:378
  (2 shorter events, 0.0 us)
Async XLA Ops:
  0.0 6.3 %copy-start.3 = (s32[128,16]{0,1:T(8,128)S(1)}, s32[128,16]{0,1:T(8,128)}, u32[]{:S(2)}) copy-start(s32[128,16]{0,1:T(8,128)} %param.20) | copy-start | bytes 24580
  0.0 6.3 %copy-start.5 = (s32[128]{0:T(128)S(1)}, s32[128]{0:T(128)}, u32[]{:S(2)}) copy-start(s32[128]{0:T(128)} %param.21) | copy-start | bytes 1540
  2.0 9.8 %all-to-all-start = ((bf16[4,16,256]{2,1,0:T(8,128)(2,1)}), bf16[4,16,256]{2,1,0:T(8,128)(2,1)S(1)}, u32[]{:S(2)}, u32[]{:S(2)}) async-start(bf16[4,16,256]{2,1,0:T(8,128)(2,1)} %get-tuple-element.14), calls=%async_computation | async-start | bytes 65536 | tf_op jit(solution)/shard_map/all_to_all | solution.py:425
  12.5 17.6 %copy-start.1 = (bf16[128,256]{1,0:T(8,128)(2,1)S(1)}, bf16[128,256]{1,0:T(8,128)(2,1)}, u32[]{:S(2)}) copy-start(bf16[128,256]{1,0:T(8,128)(2,1)} %own_a.1) | copy-start | bytes 196612
  12.6 17.6 %copy-start.2 = (bf16[64,256]{1,0:T(8,128)(2,1)S(1)}, bf16[64,256]{1,0:T(8,128)(2,1)}, u32[]{:S(2)}) copy-start(bf16[64,256]{1,0:T(8,128)(2,1)} %own_b.1) | copy-start | bytes 98308
  12.6 54.2 %all-to-all-start.1 = ((bf16[128,40,128]{2,1,0:T(8,128)(2,1)}), bf16[128,40,128]{2,1,0:T(8,128)(2,1)S(1)}, u32[]{:S(2)}, u32[]{:S(2)}) async-start(bf16[128,40,128]{2,1,0:T(8,128)(2,1)} %add_drivers.1), calls=%async_computation.1 | async-start | bytes 2621440 | tf_op jit(solution)/shard_map/all_to_all | solution.py:428
  30.1 12.9 %copy-start.6 = (s32[128]{0:T(128)S(1)}, s32[128]{0:T(128)}, u32[]{:S(2)}) copy-start(s32[128]{0:T(128)} %param.22) | copy-start | bytes 1540
  30.1 29.5 %copy-start.4 = (s32[20]{0:T(128)S(1)}, s32[20]{0:T(128)}, u32[]{:S(2)}) copy-start(s32[20]{0:T(128)} %slot_ref.1) | copy-start | bytes 244
  32.6 24.4 %collective-permute-start = (bf16[832,256]{1,0:T(8,128)(2,1)}, bf16[832,256]{1,0:T(8,128)(2,1)}, u32[]{:S(2)}, u32[]{:S(2)}) collective-permute-start(bf16[832,256]{1,0:T(8,128)(2,1)} %get-tuple-element.15), channel_id=1, source_target_pairs={{0,1},{1,2},{2,3},{3,0},{4,5},{5,6},{6,7},{7,4},{8,9},{9,10},{10,1... | collective-permute-start | bytes 1277960 | tf_op jit(solution)/shard_map/ppermute | solution.py:433
  35.1 21.9 %collective-permute-start.1 = (bf16[832,256]{1,0:T(8,128)(2,1)}, bf16[832,256]{1,0:T(8,128)(2,1)}, u32[]{:S(2)}, u32[]{:S(2)}) collective-permute-start(bf16[832,256]{1,0:T(8,128)(2,1)} %get-tuple-element.16), channel_id=1, source_target_pairs={{0,2},{1,3},{2,0},{3,1},{4,6},{5,7},{6,4},{7,5},{8,10},{9,11},{10,... | collective-permute-start | bytes 1277960 | tf_op jit(solution)/shard_map/ppermute | solution.py:433
  39.6 20.0 %collective-permute-start.2 = (bf16[832,256]{1,0:T(8,128)(2,1)}, bf16[832,256]{1,0:T(8,128)(2,1)}, u32[]{:S(2)}, u32[]{:S(2)}) collective-permute-start(bf16[832,256]{1,0:T(8,128)(2,1)} %get-tuple-element.17), channel_id=1, source_target_pairs={{0,3},{1,0},{2,1},{3,2},{4,7},{5,4},{6,5},{7,6},{8,11},{9,8},{10,9... | collective-permute-start | bytes 1277960 | tf_op jit(solution)/shard_map/ppermute | solution.py:433
  43.1 23.7 %copy-start = (bf16[2560,128]{1,0:T(8,128)(2,1)S(1)}, bf16[2560,128]{1,0:T(8,128)(2,1)}, u32[]{:S(2)}) copy-start(bf16[2560,128]{1,0:T(8,128)(2,1)} %rest_9_.1) | copy-start | bytes 1966084
